TPU v7x, 32 devices: a whole 2x2x4 slice. The times are simulated.
32 devices in a mesh: dom: 8 (over z, x), grp: 4 (over y, core).
Axes of the slice: x: 2, y: 2, z: 4, core: 2. Of those that a mesh axis runs over, the one named last changes fastest.
Arguments:
- features: bfloat16 [32768, 512], P(('dom', 'grp')), may hold values from -6 to 6
- tile_src: int32 [256, 8], P(('dom', 'grp')), may hold values from 0 to 8
- tile_val: bfloat16 [256, 8, 128, 128], P(('dom', 'grp')), may hold values from -0.1875 to 0.1875
- send_sel: int32 [32, 8], P(('dom', 'grp')), may hold values from 0 to 63
- stale_features: bfloat16 [4096, 512], P(('dom', 'grp')), may hold values from -5 to 5
- stale_grads: bfloat16 [4096, 512], P(('dom', 'grp')), may hold values from -6 to 6
- out_grad: bfloat16 [32768, 512], P(('dom', 'grp')), may hold values from -6 to 6
- master: float32 [2, 512, 512], P(None, ('dom', 'grp')), may hold values from -0.25 to 0.25
- moment_first: float32 [2, 512, 512], P(None, ('dom', 'grp')), may hold values from -0.0234375 to 0.0234375
- moment_second: float32 [2, 512, 512], P(None, ('dom', 'grp')), may hold values from 6.1035155e-07 to 1.5258789e-05
Outputs:
- layer_out: bfloat16 [32768, 512], P(('dom', 'grp'))
- fresh_features: bfloat16 [4096, 512], P(('dom', 'grp'))
- fresh_grads: bfloat16 [4096, 512], P(('dom', 'grp'))
- master_next: float32 [2, 512, 512], P(None, ('dom', 'grp'))
- weights_next: bfloat16 [2, 512, 512], replicated
Inputs may be any that keep to these rules, and one draw needn't show every extreme that they name: `tile_src`: A value below 8 names a local row block; 8 + b names boundary block b.
All inputs are finite; a program needn't handle non-finite values.
Results may differ from a plain program's by a relative error of at most 0.005.
The roundings to bfloat16 on the way count: a program that leaves them out, or rounds other values in their place, can miss the bound.
Values may be sent and summed in bfloat16 or wider, within the bound.
No kernel may reach another device: no remote copies, remote signals or barrier semaphores. Data moves between devices by JAX's collectives and lax.ppermute only.
A program may use at most 128 MiB of HBM per device.

v0:
```python
import functools

import jax
import jax.numpy as jnp
import numpy as np
from jax import lax
from jax.experimental import pallas as pl
from jax.experimental.pallas import tpu as pltpu
from jax.sharding import PartitionSpec as P


STEP = 10


decay_first = 0.9
decay_second = 0.95
learn_rate = 0.01
epsilon = 1e-08

F32 = jnp.float32
BF16 = jnp.bfloat16
AXES = ("dom", "grp")
VMEM = pl.BlockSpec(memory_space=pltpu.VMEM)
SMEM = pl.BlockSpec(memory_space=pltpu.SMEM)
ANY = pl.BlockSpec(memory_space=pl.ANY)
HBM = pl.BlockSpec(memory_space=pltpu.HBM)
PACK = 16
LAYERS = 2
GROUP = 4
BATCH = 5


def plan_stages(nd, ng):
    dom_bits = [1 << i for i in range(nd.bit_length() - 1)]
    grp_bits = [1 << i for i in range(ng.bit_length() - 1)]
    groups = [[(0, b) for b in grp_bits[:1]], [(a, 0) for a in dom_bits[:1]] + [(0, b) for b in grp_bits[1:2]]]
    rest = [(a, 0) for a in dom_bits[1:]] + [(0, b) for b in grp_bits[2:]]
    groups += [rest[i : i + 2] for i in range(0, len(rest), 2)]
    stages = []
    for bits in groups:
        members = [(0, 0)]
        for a, b in bits:
            members = members + [(a ^ x, b ^ y) for x, y in members]
        if len(members) > 1:
            stages.append(members)
    return stages


def relative_order(stages):
    order = [(0, 0)]
    for members in stages:
        order = [(a ^ x, b ^ y) for a, b in order for x, y in members]
    return order


def swap(x, mask):
    nd, ng = lax.axis_size("dom"), lax.axis_size("grp")
    pairs = [(k, ((k // ng) ^ mask[0]) * ng + ((k % ng) ^ mask[1])) for k in range(nd * ng)]
    return lax.ppermute(x, AXES, pairs)


def gather_relative(shard, stages, parts=(), ways=()):
    places = list(np.ndindex(*[len(members) for members in ways]))
    pieces = dict(zip(places, parts))
    held = shard
    for members in stages[:0:-1]:
        size = held.shape[0]
        got = [held]
        for m in members[1:]:
            lanes = [at for at in pieces for w, way in enumerate(ways) if m in way and at[w] == way.index(m)]
            came = swap(jnp.concatenate([held] + [pieces[at] for at in lanes], 0), m)
            got.append(came[:size])
            if lanes:
                pieces.update(zip(lanes, jnp.split(came[size:], len(lanes), 0)))
        held = jnp.concatenate(got, 0)
    other = swap(held, stages[0][1])
    return held, other, [pieces[at] for at in pieces]


def reduce_relative(keep, send, stages):
    got = swap(send, stages[0][1])
    total = keep.astype(F32) + got.astype(F32)
    for members in stages[1:]:
        pieces = jnp.split(total.astype(BF16), len(members), 0)
        got = [swap(p, m) for p, m in zip(pieces[1:], members[1:])]
        total = pieces[0].astype(F32)
        for g in got:
            total = total + g.astype(F32)
    return total


def dom_stages(stages):
    split = [[m for m in members if m[1] == 0] for members in stages]
    return [members for members in split if len(members) > 1]


def exchange(parts, ways, turn):
    places = list(np.ndindex(*[len(members) for members in ways]))
    held = dict(zip(places, parts))
    for s in turn:
        for i in range(1, len(ways[s])):
            lanes = [at for at in places if at[s] == i]
            got = swap(jnp.concatenate([held[at] for at in lanes], 0), ways[s][i])
            held.update(zip(lanes, jnp.split(got, len(lanes), 0)))
    return [held[at] for at in places]


class Layout:
    def __init__(self, nd, ng, shard_rows):
        self.stages = plan_stages(nd, ng)
        self.ways = dom_stages(self.stages)
        self.blocks = relative_order(self.stages)
        self.peers = [a for a, _ in relative_order(self.ways)]
        self.ng = ng
        self.packed = shard_rows % PACK == 0
        self.count = nd * ng if self.packed else nd * ng * shard_rows // PACK

    def owner(self, r):
        a, b = self.blocks[r]
        return (lax.axis_index("dom") ^ a) * self.ng + (lax.axis_index("grp") ^ b)

    def block(self, r):
        return self.owner(r) if self.packed else r

    def peer(self, r):
        return lax.axis_index("dom") ^ self.peers[r]


def dot(a, b, ca=1, cb=0):
    return lax.dot_general(a, b, (((ca,), (cb,)), ((), ())), preferred_element_type=F32)


def rows(start, size):
    return pl.ds(pl.multiple_of(start * size, size), size)


def begin_kernel(lay, sel_hbm, master_hbm, rows_ref, own_ref, out_ref, sel_ref, master_ref, sems):
    peers = len(lay.peers)
    piece = out_ref.shape[0] // peers
    sel_copy = pltpu.make_async_copy(sel_hbm, sel_ref, sems.at[peers])
    master_copy = pltpu.make_async_copy(master_hbm, master_ref, sems.at[peers + 1])
    sel_copy.start()
    master_copy.start()
    sel_copy.wait()
    copies = []
    for r in range(peers):
        src = rows_ref.at[rows(sel_ref[0, lay.peer(r)], piece), :]
        copies.append(pltpu.make_async_copy(src, out_ref.at[pl.ds(r * piece, piece), :], sems.at[r]))
    for c in copies:
        c.start()
    master_copy.wait()
    own_ref[...] = master_ref[...].astype(BF16)
    for c in copies:
        c.wait()


def prepare_kernel(src_ref, tile_ref, turned_ref, list_ref, goal_ref, count_ref):
    blocks, tiles = tile_ref.shape[:2]
    total = blocks * tiles
    slots = count_ref.shape[0]
    groups = goal_ref.shape[0]

    def turn(i, carry):
        for t in range(tiles):
            turned_ref[i * tiles + t] = tile_ref[i, t].T
        return carry

    lax.fori_loop(0, blocks, turn, 0)
    turned_ref[total] = jnp.zeros_like(turned_ref[total])
    for b in range(slots):
        count_ref[b] = 0

    def clear(k, carry):
        list_ref[k] = total
        return carry

    lax.fori_loop(0, groups * GROUP, clear, 0)

    def tally(i, carry):
        for t in range(tiles):
            b = src_ref[i, t]
            count_ref[b] = count_ref[b] + 1
        return carry

    lax.fori_loop(0, blocks, tally, 0)
    first = jnp.int32(0)
    for b in range(slots):
        need = (count_ref[b] + (GROUP - 1)) // GROUP

        def mark(g, carry, b=b):
            goal_ref[g] = b
            return carry

        lax.fori_loop(first, first + need, mark, 0)
        count_ref[b] = first * GROUP
        first = first + need

    def rest(g, carry):
        goal_ref[g] = 0
        return carry

    lax.fori_loop(first, groups, rest, 0)
    goal_ref[groups - 1] = first

    def enter(i, carry):
        for t in range(tiles):
            b = src_ref[i, t]
            at = count_ref[b]
            list_ref[at] = i * tiles + t
            count_ref[b] = at + 1
        return carry

    lax.fori_loop(0, blocks, enter, 0)


def aggregate_block(i, src_ref, tile_ref, table_ref):
    tiles, edge = tile_ref.shape[1], tile_ref.shape[2]
    left = jnp.concatenate([tile_ref[i, t] for t in range(tiles)], 1)
    right = jnp.concatenate([table_ref[rows(src_ref[i, t], edge), :] for t in range(tiles)], 0)
    return dot(left, right).astype(BF16)


def first_kernel(lay, src_ref, feat_ref, rim_ref, tile_ref, out_ref, turned_ref, table_ref):
    blocks, edge = tile_ref.shape[0], tile_ref.shape[2]
    local = feat_ref.shape[0]
    peers = len(lay.peers)
    piece = rim_ref.shape[0] // peers
    table_ref[:local, :] = feat_ref[...]
    for r in range(peers):
        at = pl.multiple_of(local + lay.peer(r) * piece, piece)
        table_ref[pl.ds(at, piece), :] = rim_ref[r * piece : (r + 1) * piece, :]
    for i in range(blocks):
        out = aggregate_block(i, src_ref, tile_ref, table_ref)
        out_ref[i * edge : (i + 1) * edge, :] = out
        turned_ref[:, i * edge : (i + 1) * edge] = out.T


def assemble(lay, dst_ref, parts, layer):
    size = dst_ref.shape[0] // lay.count
    half = lay.count // len(parts)
    for r in range(lay.count):
        at = ((r % half) * LAYERS + layer) * size
        dst_ref[rows(lay.block(r), size), :] = parts[r // half][at : at + size, :]


def scatter_grad(lay, full_ref, outs, layer):
    size = full_ref.shape[0] // lay.count
    half = lay.count // len(outs)
    for r in range(lay.count):
        at = ((r % half) * LAYERS + layer) * size
        outs[r // half][at : at + size, :] = full_ref[rows(lay.block(r), size), :].astype(BF16)


def spread_kernel(lay, list_ref, goal_ref, sel_ref, og_ref, turned_ref, lo_ref, hi_ref, stale_ref, acc_ref, w_ref, up_ref):
    edge = turned_ref.shape[1]
    blocks = og_ref.shape[0] // edge
    tiles = (turned_ref.shape[0] - 1) // blocks
    peers = len(lay.peers)
    piece = stale_ref.shape[0] // peers
    assemble(lay, w_ref, (lo_ref, hi_ref), 1)
    acc_ref[...] = jnp.zeros_like(acc_ref)
    for i in range(blocks):
        at = slice(i * edge, (i + 1) * edge)
        up_ref[at, :] = dot(og_ref[at, :], w_ref[...], 1, 1).astype(BF16)

    def body(n, carry):
        sums = []
        for u in range(BATCH):
            g = n * BATCH + u
            ks = [list_ref[g * GROUP + j] for j in range(GROUP)]
            left = jnp.concatenate([turned_ref[k] for k in ks], 1)
            right = jnp.concatenate([up_ref[rows(jnp.minimum(k // tiles, blocks - 1), edge), :] for k in ks], 0)
            sums.append((rows(goal_ref[g], edge), dot(left, right)))
        for at, part in sums:
            acc_ref[at, :] += part
        return carry

    used = goal_ref[goal_ref.shape[0] - 1]
    lax.fori_loop(0, (used + (BATCH - 1)) // BATCH, body, 0)
    for p in range(peers):
        at = rows(sel_ref[p], piece)
        acc_ref[at, :] += stale_ref[p * piece : (p + 1) * piece, :].astype(F32)


def hidden_kernel(lay, sel_ref, p_ref, turned_ref, acc_ref, lo_ref, hi_ref, h_ref, route_ref, full_ref, w_ref, dz_ref):
    step = 128
    local = p_ref.shape[0]
    peers = len(lay.peers)
    piece = (acc_ref.shape[0] - local) // peers
    assemble(lay, w_ref, (lo_ref, hi_ref), 0)
    for i in range(local // step):
        at = slice(i * step, (i + 1) * step)
        z = dot(p_ref[at, :], w_ref[...])
        s = 1.0 / (1.0 + jnp.exp(-z))
        h_ref[at, :] = (z * s).astype(BF16)
        dz_ref[at, :] = (acc_ref[at, :] * s * (1.0 + z * (1.0 - s))).astype(BF16)
    for m in range(full_ref.shape[0] // step):
        at = slice(m * step, (m + 1) * step)
        full_ref[at, :] = dot(turned_ref[at, :], dz_ref[...])
    for r in range(peers):
        q = lay.peer(r)
        at = 2 * r * piece
        route_ref[at : at + piece, :] = h_ref[rows(sel_ref[q], piece), :]
        back = acc_ref[pl.ds(pl.multiple_of(local + q * piece, piece), piece), :]
        route_ref[at + piece : at + 2 * piece, :] = back.astype(BF16)


def second_kernel(lay, src_ref, h_ref, rim_ref, tile_ref, og_ref, first_ref, p_ref, keep_ref, send_ref, table_ref, full_ref):
    blocks, edge = tile_ref.shape[0], tile_ref.shape[2]
    step = 128
    local = h_ref.shape[0]
    table_ref[:local, :] = h_ref[...]
    table_ref[local:, :] = rim_ref[...]
    for i in range(blocks):
        p_ref[i * edge : (i + 1) * edge, :] = aggregate_block(i, src_ref, tile_ref, table_ref)
    for m in range(full_ref.shape[0] // step):
        cols = slice(m * step, (m + 1) * step)
        full_ref[cols, :] = dot(p_ref[:, cols], og_ref[...], 0, 0)
    scatter_grad(lay, first_ref, (keep_ref, send_ref), 0)
    scatter_grad(lay, full_ref, (keep_ref, send_ref), 1)


def out_kernel(lay, p_ref, lo_ref, hi_ref, out_ref, w_ref):
    step = 128
    assemble(lay, w_ref, (lo_ref, hi_ref), 1)
    for i in range(p_ref.shape[0] // step):
        at = slice(i * step, (i + 1) * step)
        out_ref[at, :] = dot(p_ref[at, :], w_ref[...]).astype(BF16)


def place_rows(lay, half_at, part_ref, out_ref):
    half = lay.count // 2
    size = out_ref.shape[1] // lay.count
    for r in range(half):
        for layer in range(LAYERS):
            src = part_ref.at[pl.ds((r * LAYERS + layer) * size, size), :]
            yield src, out_ref.at[layer, rows(lay.block(half_at * half + r), size), :]


def place_fresh(lay, fresh_ref, feat_ref, grad_ref):
    piece = feat_ref.shape[0] // len(lay.peers)
    for r in range(len(lay.peers)):
        at = rows(lay.peer(r), piece)
        yield fresh_ref.at[pl.ds(2 * r * piece, piece), :], feat_ref.at[at, :]
        yield fresh_ref.at[pl.ds((2 * r + 1) * piece, piece), :], grad_ref.at[at, :]


def run_copies(pairs, sems):
    copies = [pltpu.make_async_copy(src, dst, sems.at[n]) for n, (src, dst) in enumerate(pairs)]
    for c in copies:
        c.start()
    for c in copies:
        c.wait()


def place_kernel(lay, part_ref, fresh_ref, out_ref, feat_ref, grad_ref, sems):
    pairs = [*place_rows(lay, 0, part_ref, out_ref), *place_fresh(lay, fresh_ref, feat_ref, grad_ref)]
    run_copies(pairs, sems)


def finish_kernel(lay, part_ref, held_ref, out_ref, sems):
    run_copies(place_rows(lay, 1, part_ref, out_ref), sems)


def call(body, out_shape, specs, out_specs, scratch, flops, moved, aliases=None):
    return pl.pallas_call(
        body,
        out_shape=out_shape,
        in_specs=specs,
        out_specs=out_specs,
        scratch_shapes=scratch,
        input_output_aliases=aliases or {},
        cost_estimate=pl.CostEstimate(flops=flops, bytes_accessed=moved, transcendentals=0),
        compiler_params=pltpu.CompilerParams(vmem_limit_bytes=40 * 1024 * 1024),
    )


def epoch(
    features,
    tile_src,
    tile_val,
    send_sel,
    stale_features,
    stale_grads,
    out_grad,
    master,
    moment_first,
    moment_second,
):
    peers = lax.axis_size("dom")
    groups = lax.axis_size("grp")
    devices = peers * groups
    local, width = features.shape
    total_nodes = local * devices
    blocks, tiles, edge = tile_val.shape[:3]
    rim = stale_features.shape[0]
    layers, shard_rows = master.shape[:2]
    full_rows = shard_rows * devices
    slots = blocks + rim // edge
    selects = send_sel[0]
    lay = Layout(peers, groups, shard_rows)
    count, size = lay.count, full_rows // lay.count
    half = layers * full_rows // 2
    sds = jax.ShapeDtypeStruct

    def spread_out(lo, hi):
        if lay.packed:
            return lo, hi
        owner = jnp.stack([lay.owner(r) for r in range(devices)])
        inverse = jnp.argmax(owner[None, :] == jnp.arange(devices, dtype=jnp.int32)[:, None], axis=1)
        whole = jnp.concatenate((lo, hi), 0).reshape(devices, layers, shard_rows, width)
        whole = jnp.take(whole, inverse, axis=0).transpose(1, 0, 2, 3).reshape(layers, count, size, width)
        whole = whole.transpose(1, 0, 2, 3).reshape(layers * full_rows, width)
        return whole[:half], whole[half:]

    def draw_in(keep, send):
        if lay.packed:
            return keep, send
        owner = jnp.stack([lay.owner(r) for r in range(devices)])
        whole = jnp.concatenate((keep, send), 0).reshape(count, layers, size, width).transpose(1, 0, 2, 3)
        whole = whole.reshape(layers, devices, shard_rows, width).transpose(1, 0, 2, 3)
        whole = jnp.take(whole, owner, axis=0).reshape(layers * full_rows, width)
        return whole[:half], whole[half:]

    tile_flops = 2 * blocks * tiles * edge * edge * width
    dense_flops = 2 * local * width * width
    tile_bytes = tile_val.size * 2
    node_bytes = features.size * 2
    nodes = sds((local, width), BF16)
    square = sds((full_rows, width), F32)
    grads_half = sds((half, width), BF16)
    listed = -(-(blocks * tiles + slots * (GROUP - 1)) // GROUP)
    listed = -(-listed // BATCH) * BATCH + 1
    part = functools.partial

    own, picked = call(
        part(begin_kernel, lay),
        (sds(master.shape, BF16), sds((rim, width), BF16)),
        [HBM, HBM, HBM],
        (VMEM, VMEM),
        [
            pltpu.SMEM((1, peers), jnp.int32),
            pltpu.VMEM(master.shape, F32),
            pltpu.SemaphoreType.DMA((peers + 2,)),
        ],
        0,
        rim * width * 4,
    )(*(pltpu.with_memory_space_constraint(x, pltpu.HBM) for x in (send_sel, master, features)))
    lo, hi, raw_rim = gather_relative(
        own.reshape(layers * shard_rows, width), lay.stages, jnp.split(picked, peers, 0), lay.ways
    )
    lo, hi = spread_out(lo, hi)
    raw_rim = jnp.concatenate(raw_rim, 0)
    turned_tiles, order, goal = call(
        prepare_kernel,
        (
            sds((blocks * tiles + 1, edge, edge), BF16),
            sds((listed * GROUP,), jnp.int32),
            sds((listed,), jnp.int32),
        ),
        [SMEM, VMEM],
        (VMEM, SMEM, SMEM),
        [pltpu.SMEM((slots,), jnp.int32)],
        0,
        2 * tile_bytes,
    )(tile_src, tile_val)
    p_first, p_turned = call(
        part(first_kernel, lay),
        (nodes, sds((width, local), BF16)),
        [SMEM, VMEM, VMEM, VMEM],
        (VMEM, VMEM),
        [pltpu.VMEM((local + rim, width), BF16)],
        tile_flops,
        tile_bytes + 2 * node_bytes,
    )(tile_src, features, raw_rim, tile_val)
    acc = call(
        part(spread_kernel, lay),
        sds((local + rim, width), F32),
        [SMEM, SMEM, SMEM, VMEM, VMEM, VMEM, VMEM, VMEM],
        VMEM,
        [pltpu.VMEM((full_rows, width), BF16), pltpu.VMEM((local, width), BF16)],
        tile_flops + dense_flops,
        tile_bytes + 3 * node_bytes,
    )(order, goal, selects, out_grad, turned_tiles, lo, hi, stale_grads)
    h_first, route, g_first = call(
        part(hidden_kernel, lay),
        (nodes, sds((2 * rim, width), BF16), square),
        [SMEM, VMEM, VMEM, VMEM, VMEM, VMEM],
        (VMEM, VMEM, VMEM),
        [pltpu.VMEM((full_rows, width), BF16), pltpu.VMEM((local, width), BF16)],
        2 * dense_flops,
        4 * node_bytes,
    )(selects, p_first, p_turned, acc, lo, hi)
    p_second, keep, send = call(
        part(second_kernel, lay),
        (nodes, grads_half, grads_half),
        [SMEM, VMEM, VMEM, VMEM, VMEM, VMEM],
        (VMEM, VMEM, VMEM),
        [pltpu.VMEM((local + rim, width), BF16), pltpu.VMEM((full_rows, width), F32)],
        tile_flops + dense_flops,
        tile_bytes + 3 * node_bytes,
    )(tile_src, h_first, stale_features, tile_val, out_grad, g_first)
    shard = reduce_relative(*draw_in(keep, send), lay.stages).reshape(layers, shard_rows, width) / total_nodes
    layer_out = call(
        part(out_kernel, lay),
        nodes,
        [VMEM, VMEM, VMEM],
        VMEM,
        [pltpu.VMEM((full_rows, width), BF16)],
        dense_flops,
        2 * node_bytes,
    )(p_second, lo, hi)
    fresh = jnp.concatenate(exchange(jnp.split(route, peers, 0), lay.ways, range(len(lay.ways))[::-1]), 0)

    moment_new = decay_first * moment_first + (1.0 - decay_first) * shard
    second_new = decay_second * moment_second + (1.0 - decay_second) * shard * shard
    update = moment_new / (1.0 - decay_first**STEP) / (jnp.sqrt(second_new / (1.0 - decay_second**STEP)) + epsilon)
    master_next = master - learn_rate * update
    moved = master_next.astype(BF16).reshape(layers * shard_rows, width)
    lo_next, hi_next, _ = gather_relative(moved, lay.stages)
    lo_next, hi_next = spread_out(lo_next, hi_next)
    weights = sds((layers, full_rows, width), BF16)
    weights_next, fresh_features, fresh_grads = call(
        part(place_kernel, lay),
        (weights, sds((rim, width), BF16), sds((rim, width), BF16)),
        [VMEM, VMEM],
        (HBM, HBM, HBM),
        [pltpu.SemaphoreType.DMA((layers * count // 2 + 2 * peers,))],
        0,
        2 * layers * full_rows * width,
    )(lo_next, fresh)
    weights_next = call(
        part(finish_kernel, lay),
        weights,
        [VMEM, HBM],
        HBM,
        [pltpu.SemaphoreType.DMA((layers * count // 2,))],
        0,
        2 * layers * full_rows * width,
        aliases={1: 0},
    )(hi_next, weights_next)
    return (layer_out, fresh_features, fresh_grads, master_next, weights_next)


def solution(mesh):
    placed = (
        P(("dom", "grp"), None),
        P(("dom", "grp"), None),
        P(("dom", "grp"), None, None, None),
        P(("dom", "grp"), None),
        P(("dom", "grp"), None),
        P(("dom", "grp"), None),
        P(("dom", "grp"), None),
        P(None, ("dom", "grp"), None),
        P(None, ("dom", "grp"), None),
        P(None, ("dom", "grp"), None),
    )
    return jax.shard_map(
        epoch,
        mesh=mesh,
        in_specs=placed,
        out_specs=(
            P(("dom", "grp"), None),
            P(("dom", "grp"), None),
            P(("dom", "grp"), None),
            P(None, ("dom", "grp"), None),
            P(),
        ),
        check_vma=False,
    )
```

profile of v0, /device:TPU:0, one launch (start us, length us, event | category | flops | bytes accessed | tf_op | source)
XLA Modules:
  0.0 85.2 jit_solution(15116489918582133799)
XLA Ops:
  0.7 1.7 %shard_map.137 = (bf16[2,16,512]{2,1,0:T(8,128)(2,1)S(1)}, bf16[128,512]{1,0:T(8,128)(2,1)S(1)}) custom-call(s32[1,8]{1,0:T(1,128)} %sel_hbm.1, f32[2,16,512]{2,1,0:T(8,128)} %master_hbm.1, bf16[1024,512]{1,0:T(8,128)(2,1)} %feat_ref.1), custom_call_target="tpu_custom_call" | custom-call | bytes 262144 | tf_op jit(solution)/shard_map/pallas_call | solution.py:436
  2.5 5.1 %collective-permute-start.2 = (bf16[64,512]{1,0:T(8,128)(2,1)S(1)}, bf16[64,512]{1,0:T(8,128)(2,1)S(1)}, u32[]{:S(2)}, u32[]{:S(2)}) collective-permute-start(bf16[64,512]{1,0:T(8,128)(2,1)S(1)} %get-tuple-element.86), channel_id=1, source_target_pairs={{0,24},{1,25},{2,26},{3,27},{4,28},{5,29},{6,30},{7,31},{8,16},{9,... | collective-permute-start | bytes 196616 | tf_op jit(solution)/shard_map/ppermute | solution.py:59
  8.2 3.6 %collective-permute-done = bf16[64,512]{1,0:T(8,128)(2,1)S(1)} collective-permute-done((bf16[64,512]{1,0:T(8,128)(2,1)S(1)}, bf16[64,512]{1,0:T(8,128)(2,1)S(1)}, u32[]{:S(2)}, u32[]{:S(2)}) %collective-permute-start) | collective-permute-done | bytes 65568 | tf_op jit(solution)/shard_map/ppermute | solution.py:59
  11.9 1.3 %collective-permute-done.1 = bf16[64,512]{1,0:T(8,128)(2,1)S(1)} collective-permute-done((bf16[64,512]{1,0:T(8,128)(2,1)S(1)}, bf16[64,512]{1,0:T(8,128)(2,1)S(1)}, u32[]{:S(2)}, u32[]{:S(2)}) %collective-permute-start.1) | collective-permute-done | bytes 65568 | tf_op jit(solution)/shard_map/ppermute | solution.py:59
  13.3 1.6 %collective-permute-start.3 = (bf16[192,512]{1,0:T(8,128)(2,1)S(1)}, bf16[192,512]{1,0:T(8,128)(2,1)S(1)}, u32[]{:S(2)}, u32[]{:S(2)}) collective-permute-start(bf16[192,512]{1,0:T(8,128)(2,1)S(1)} %get-tuple-element.78), channel_id=1, source_target_pairs={{0,4},{1,5},{2,6},{3,7},{4,0},{5,1},{6,2},{7,3},{8,12},{9,13},{10,... | collective-permute-start | bytes 589832 | tf_op jit(solution)/shard_map/ppermute | solution.py:59
  14.9 1.6 %collective-permute-start.5 = (bf16[128,512]{1,0:T(8,128)(2,1)S(1)}, bf16[128,512]{1,0:T(8,128)(2,1)S(1)}, u32[]{:S(2)}, u32[]{:S(2)}) collective-permute-start(bf16[128,512]{1,0:T(8,128)(2,1)S(1)} %pad_maximum_fusion), channel_id=1, source_target_pairs={{0,6},{1,7},{2,4},{3,5},{4,2},{5,3},{6,0},{7,1},{8,14},{9,15},{10,... | collective-permute-start | bytes 393224 | tf_op jit(solution)/shard_map/ppermute | solution.py:59
  16.9 4.2 %collective-permute-done.3 = bf16[192,512]{1,0:T(8,128)(2,1)S(1)} collective-permute-done((bf16[192,512]{1,0:T(8,128)(2,1)S(1)}, bf16[192,512]{1,0:T(8,128)(2,1)S(1)}, u32[]{:S(2)}, u32[]{:S(2)}) %collective-permute-start.3) | collective-permute-done | bytes 196640 | tf_op jit(solution)/shard_map/ppermute | solution.py:59
  21.1 2.9 %collective-permute-done.4 = bf16[128,512]{1,0:T(8,128)(2,1)S(1)} collective-permute-done((bf16[128,512]{1,0:T(8,128)(2,1)S(1)}, bf16[128,512]{1,0:T(8,128)(2,1)S(1)}, u32[]{:S(2)}, u32[]{:S(2)}) %collective-permute-start.4) | collective-permute-done | bytes 131104 | tf_op jit(solution)/shard_map/ppermute | solution.py:59
  24.2 3.7 %shard_map.139 = (bf16[65,128,128]{2,1,0:T(8,128)(2,1)S(1)}, s32[104]{0:T(128)S(1)}, s32[26]{0:T(128)S(1)}) custom-call(s32[8,8]{1,0:T(8,128)S(1)} %copy-done.5, bf16[8,8,128,128]{3,2,1,0:T(8,128)(2,1)S(1)} %copy-done), custom_call_target="tpu_custom_call" | custom-call | bytes 4194304 | tf_op jit(solution)/shard_map/pallas_call | solution.py:454
  28.0 2.1 %shard_map.138 = (bf16[1024,512]{1,0:T(8,128)(2,1)S(1)}, bf16[512,1024]{1,0:T(8,128)(2,1)S(1)}) custom-call(s32[8,8]{1,0:T(8,128)S(1)} %copy-done.5, bf16[1024,512]{1,0:T(8,128)(2,1)S(1)} %copy-done.1, bf16[128,512]{1,0:T(8,128)(2,1)S(1)} %constant_dynamic-update-slice_fusion.8.rim_ref, bf16[8,8,128,128]{3,2,1,0:T(8,128)(2,1)S(1)} %copy-done), custom_call_target="tpu_custom_call" | custom-call | flops 1073741824 | bytes 4194304 | tf_op jit(solution)/shard_map/pallas_call | solution.py:467
  30.2 4.6 %shard_map.140.acc_ref = f32[1152,512]{1,0:T(8,128)S(1)} custom-call(s32[104]{0:T(128)S(1)} %get-tuple-element.25.list_ref, s32[26]{0:T(128)S(1)} %get-tuple-element.26.goal_ref, s32[8]{0:T(128)S(1)} %bitcast.8, bf16[1024,512]{1,0:T(8,128)(2,1)S(1)} %copy-done.2, bf16[65,128,128]{2,1,0:T(8,128)(2,1)S(1)} %get-tuple-element.27.turned_ref, ...), custom_call_target="tpu_custom_call" | custom-call | flops 1610612736 | bytes 5242880 | tf_op jit(solution)/shard_map/pallas_call | solution.py:476
  34.8 2.5 %shard_map.141 = (bf16[1024,512]{1,0:T(8,128)(2,1)S(1)}, bf16[256,512]{1,0:T(8,128)(2,1)S(1)}, f32[512,512]{1,0:T(8,128)S(1)}) custom-call(s32[8]{0:T(128)S(1)} %bitcast.9, bf16[1024,512]{1,0:T(8,128)(2,1)S(1)} %get-tuple-element.23.p_ref, bf16[512,1024]{1,0:T(8,128)(2,1)S(1)} %get-tuple-element.24.turned_ref, f32[1152,512]{1,0:T(8,128)S(1)} %shard_map.140.acc_ref, ...), custom_call_target="tpu_custom_call" | custom-call | flops 1073741824 | bytes 4194304 | tf_op jit(solution)/shard_map/pallas_call | solution.py:485
  37.3 2.8 %shard_map.142 = (bf16[1024,512]{1,0:T(8,128)(2,1)S(1)}, bf16[512,512]{1,0:T(8,128)(2,1)S(1)}, bf16[512,512]{1,0:T(8,128)(2,1)S(1)}) custom-call(s32[8,8]{1,0:T(8,128)S(1)} %copy-done.5, bf16[1024,512]{1,0:T(8,128)(2,1)S(1)} %get-tuple-element.28.h_ref, bf16[128,512]{1,0:T(8,128)(2,1)S(1)} %copy-done.6, bf16[8,8,128,128]{3,2,1,0:T(8,128)(2,1)S(1)} %copy-done, ...), custom_call_target="tpu_custom_call" | custom-call | flops 1610612736 | bytes 5242880 | tf_op jit(solution)/shard_map/pallas_call | solution.py:494
  40.8 2.0 %collective-permute-start.21 = (bf16[64,512]{1,0:T(8,128)(2,1)S(1)}, bf16[64,512]{1,0:T(8,128)(2,1)S(1)}, u32[]{:S(2)}, u32[]{:S(2)}) collective-permute-start(bf16[64,512]{1,0:T(8,128)(2,1)S(1)} %pad_maximum_fusion.7), channel_id=1, source_target_pairs={{0,16},{1,17},{2,18},{3,19},{4,20},{5,21},{6,22},{7,23},{8,24},{9,... | collective-permute-start | bytes 196616 | tf_op jit(solution)/shard_map/ppermute | solution.py:59
  42.9 2.3 %collective-permute-start.22 = (bf16[64,512]{1,0:T(8,128)(2,1)S(1)}, bf16[64,512]{1,0:T(8,128)(2,1)S(1)}, u32[]{:S(2)}, u32[]{:S(2)}) collective-permute-start(bf16[64,512]{1,0:T(8,128)(2,1)S(1)} %pad_maximum_fusion.8), channel_id=1, source_target_pairs={{0,24},{1,25},{2,26},{3,27},{4,28},{5,29},{6,30},{7,31},{8,16},{9,... | collective-permute-start | bytes 196616 | tf_op jit(solution)/shard_map/ppermute | solution.py:59
  45.4 1.6 %collective-permute-start.8 = (bf16[128,512]{1,0:T(8,128)(2,1)S(1)}, bf16[128,512]{1,0:T(8,128)(2,1)S(1)}, u32[]{:S(2)}, u32[]{:S(2)}) collective-permute-start(bf16[128,512]{1,0:T(8,128)(2,1)S(1)} %get-tuple-element.39), channel_id=1, source_target_pairs={{0,4},{1,5},{2,6},{3,7},{4,0},{5,1},{6,2},{7,3},{8,12},{9,13},{10,... | collective-permute-start | bytes 393224 | tf_op jit(solution)/shard_map/ppermute | solution.py:59
  47.3 1.6 %collective-permute-start.9 = (bf16[128,512]{1,0:T(8,128)(2,1)S(1)}, bf16[128,512]{1,0:T(8,128)(2,1)S(1)}, u32[]{:S(2)}, u32[]{:S(2)}) collective-permute-start(bf16[128,512]{1,0:T(8,128)(2,1)S(1)} %get-tuple-element.41), channel_id=1, source_target_pairs={{0,2},{1,3},{2,0},{3,1},{4,6},{5,7},{6,4},{7,5},{8,10},{9,11},{10,... | collective-permute-start | bytes 393224 | tf_op jit(solution)/shard_map/ppermute | solution.py:59
  48.9 2.5 %collective-permute-done.8 = bf16[128,512]{1,0:T(8,128)(2,1)S(1)} collective-permute-done((bf16[128,512]{1,0:T(8,128)(2,1)S(1)}, bf16[128,512]{1,0:T(8,128)(2,1)S(1)}, u32[]{:S(2)}, u32[]{:S(2)}) %collective-permute-start.8) | collective-permute-done | bytes 131104 | tf_op jit(solution)/shard_map/ppermute | solution.py:59
  51.4 1.7 %collective-permute-done.10 = bf16[128,512]{1,0:T(8,128)(2,1)S(1)} collective-permute-done((bf16[128,512]{1,0:T(8,128)(2,1)S(1)}, bf16[128,512]{1,0:T(8,128)(2,1)S(1)}, u32[]{:S(2)}, u32[]{:S(2)}) %collective-permute-start.10) | collective-permute-done | bytes 131104 | tf_op jit(solution)/shard_map/ppermute | solution.py:59
  53.1 1.2 %collective-permute-done.9 = bf16[128,512]{1,0:T(8,128)(2,1)S(1)} collective-permute-done((bf16[128,512]{1,0:T(8,128)(2,1)S(1)}, bf16[128,512]{1,0:T(8,128)(2,1)S(1)}, u32[]{:S(2)}, u32[]{:S(2)}) %collective-permute-start.9) | collective-permute-done | bytes 131104 | tf_op jit(solution)/shard_map/ppermute | solution.py:59
  54.5 2.2 %collective-permute-start.13 = (bf16[32,512]{1,0:T(8,128)(2,1)S(1)}, bf16[32,512]{1,0:T(8,128)(2,1)S(1)}, u32[]{:S(2)}, u32[]{:S(2)}) collective-permute-start(bf16[32,512]{1,0:T(8,128)(2,1)S(1)} %get-tuple-element.53), channel_id=1, source_target_pairs={{0,24},{1,25},{2,26},{3,27},{4,28},{5,29},{6,30},{7,31},{8,16},{9,... | collective-permute-start | bytes 98312 | tf_op jit(solution)/shard_map/ppermute | solution.py:59
  56.7 1.2 %collective-permute-start.12 = (bf16[32,512]{1,0:T(8,128)(2,1)S(1)}, bf16[32,512]{1,0:T(8,128)(2,1)S(1)}, u32[]{:S(2)}, u32[]{:S(2)}) collective-permute-start(bf16[32,512]{1,0:T(8,128)(2,1)S(1)} %get-tuple-element.54), channel_id=1, source_target_pairs={{0,16},{1,17},{2,18},{3,19},{4,20},{5,21},{6,22},{7,23},{8,24},{9,... | collective-permute-start | bytes 98312 | tf_op jit(solution)/shard_map/ppermute | solution.py:59
  58.4 1.9 %collective-permute-done.13 = bf16[32,512]{1,0:T(8,128)(2,1)S(1)} collective-permute-done((bf16[32,512]{1,0:T(8,128)(2,1)S(1)}, bf16[32,512]{1,0:T(8,128)(2,1)S(1)}, u32[]{:S(2)}, u32[]{:S(2)}) %collective-permute-start.13) | collective-permute-done | bytes 32800 | tf_op jit(solution)/shard_map/ppermute | solution.py:59
  60.3 1.3 %collective-permute-done.12 = bf16[32,512]{1,0:T(8,128)(2,1)S(1)} collective-permute-done((bf16[32,512]{1,0:T(8,128)(2,1)S(1)}, bf16[32,512]{1,0:T(8,128)(2,1)S(1)}, u32[]{:S(2)}, u32[]{:S(2)}) %collective-permute-start.12) | collective-permute-done | bytes 32800 | tf_op jit(solution)/shard_map/ppermute | solution.py:59
  62.3 1.6 %collective-permute-start.16 = (bf16[32,512]{1,0:T(8,128)(2,1)S(1)}, bf16[32,512]{1,0:T(8,128)(2,1)S(1)}, u32[]{:S(2)}, u32[]{:S(2)}) collective-permute-start(bf16[32,512]{1,0:T(8,128)(2,1)S(1)} %bitcast.10), channel_id=1, source_target_pairs={{0,24},{1,25},{2,26},{3,27},{4,28},{5,29},{6,30},{7,31},{8,16},{9,... | collective-permute-start | bytes 98312 | tf_op jit(solution)/shard_map/ppermute | solution.py:59
  64.8 1.9 %collective-permute-start.14 = (bf16[32,512]{1,0:T(8,128)(2,1)S(1)}, bf16[32,512]{1,0:T(8,128)(2,1)S(1)}, u32[]{:S(2)}, u32[]{:S(2)}) collective-permute-start(bf16[32,512]{1,0:T(8,128)(2,1)S(1)} %bitcast.12), channel_id=1, source_target_pairs={{0,8},{1,9},{2,10},{3,11},{4,12},{5,13},{6,14},{7,15},{8,0},{9,1},... | collective-permute-start | bytes 98312 | tf_op jit(solution)/shard_map/ppermute | solution.py:59
  66.7 1.3 %collective-permute-done.16 = bf16[32,512]{1,0:T(8,128)(2,1)S(1)} collective-permute-done((bf16[32,512]{1,0:T(8,128)(2,1)S(1)}, bf16[32,512]{1,0:T(8,128)(2,1)S(1)}, u32[]{:S(2)}, u32[]{:S(2)}) %collective-permute-start.16) | collective-permute-done | bytes 32800 | tf_op jit(solution)/shard_map/ppermute | solution.py:59
  69.1 2.1 %collective-permute-start.19 = (bf16[128,512]{1,0:T(8,128)(2,1)S(1)}, bf16[128,512]{1,0:T(8,128)(2,1)S(1)}, u32[]{:S(2)}, u32[]{:S(2)}) collective-permute-start(bf16[128,512]{1,0:T(8,128)(2,1)S(1)} %pad_maximum_fusion.1), channel_id=1, source_target_pairs={{0,6},{1,7},{2,4},{3,5},{4,2},{5,3},{6,0},{7,1},{8,14},{9,15},{10,... | collective-permute-start | bytes 393224 | tf_op jit(solution)/shard_map/ppermute | solution.py:59
  72.6 4.0 %collective-permute-done.17 = bf16[128,512]{1,0:T(8,128)(2,1)S(1)} collective-permute-done((bf16[128,512]{1,0:T(8,128)(2,1)S(1)}, bf16[128,512]{1,0:T(8,128)(2,1)S(1)}, u32[]{:S(2)}, u32[]{:S(2)}) %collective-permute-start.17) | collective-permute-done | bytes 131104 | tf_op jit(solution)/shard_map/ppermute | solution.py:59
  77.9 1.8 %shard_map.143 = bf16[1024,512]{1,0:T(8,128)(2,1)} custom-call(bf16[1024,512]{1,0:T(8,128)(2,1)S(1)} %get-tuple-element.30.p_ref, bf16[512,512]{1,0:T(8,128)(2,1)S(1)} %constant_dynamic-update-slice_fusion.13.lo_ref, bf16[512,512]{1,0:T(8,128)(2,1)S(1)} %collective-permute-done.6.hi_ref), custom_call_target="tpu_custom_call" | custom-call | flops 536870912 | bytes 2097152 | tf_op jit(solution)/shard_map/pallas_call | solution.py:504
  79.6 3.1 %collective-permute-done.23 = bf16[128,512]{1,0:T(8,128)(2,1)S(1)} collective-permute-done((bf16[128,512]{1,0:T(8,128)(2,1)S(1)}, bf16[128,512]{1,0:T(8,128)(2,1)S(1)}, u32[]{:S(2)}, u32[]{:S(2)}) %collective-permute-start.23) | collective-permute-done | bytes 131104 | tf_op jit(solution)/shard_map/ppermute | solution.py:59
  82.8 1.3 %shard_map.144 = (bf16[2,512,512]{2,1,0:T(8,128)(2,1)}, bf16[128,512]{1,0:T(8,128)(2,1)}, bf16[128,512]{1,0:T(8,128)(2,1)}) custom-call(bf16[512,512]{1,0:T(8,128)(2,1)S(1)} %constant_dynamic-update-slice_fusion.19.part_ref, bf16[256,512]{1,0:T(8,128)(2,1)S(1)} %constant_dynamic-update-slice_fusion.26.fresh_ref), custom_call_target="tpu_custom_call" | custom-call | bytes 1048576 | tf_op jit(solution)/shard_map/pallas_call | solution.py:523
  (85 shorter events, 9.6 us)
Async XLA Ops:
  0.6 23.6 %copy-start = (bf16[8,8,128,128]{3,2,1,0:T(8,128)(2,1)S(1)}, bf16[8,8,128,128]{3,2,1,0:T(8,128)(2,1)}, u32[]{:S(2)}) copy-start(bf16[8,8,128,128]{3,2,1,0:T(8,128)(2,1)} %tile_ref.5) | copy-start | bytes 6291460
  0.6 23.6 %copy-start.5 = (s32[8,8]{1,0:T(8,128)S(1)}, s32[8,8]{1,0:T(8,128)}, u32[]{:S(2)}) copy-start(s32[8,8]{1,0:T(8,128)} %src_ref.5) | copy-start | bytes 772
  2.4 25.5 %copy-start.1 = (bf16[1024,512]{1,0:T(8,128)(2,1)S(1)}, bf16[1024,512]{1,0:T(8,128)(2,1)}, u32[]{:S(2)}) copy-start(bf16[1024,512]{1,0:T(8,128)(2,1)} %feat_ref.1) | copy-start | bytes 3145732
  2.5 10.8 %collective-permute-start.2 = (bf16[64,512]{1,0:T(8,128)(2,1)S(1)}, bf16[64,512]{1,0:T(8,128)(2,1)S(1)}, u32[]{:S(2)}, u32[]{:S(2)}) collective-permute-start(bf16[64,512]{1,0:T(8,128)(2,1)S(1)} %get-tuple-element.86), channel_id=1, source_target_pairs={{0,24},{1,25},{2,26},{3,27},{4,28},{5,29},{6,30},{7,31},{8,16},{9,... | collective-permute-start | bytes 196616 | tf_op jit(solution)/shard_map/ppermute | solution.py:59
  7.6 5.6 %collective-permute-start.1 = (bf16[64,512]{1,0:T(8,128)(2,1)S(1)}, bf16[64,512]{1,0:T(8,128)(2,1)S(1)}, u32[]{:S(2)}, u32[]{:S(2)}) collective-permute-start(bf16[64,512]{1,0:T(8,128)(2,1)S(1)} %get-tuple-element.87), channel_id=1, source_target_pairs={{0,16},{1,17},{2,18},{3,19},{4,20},{5,21},{6,22},{7,23},{8,24},{9,... | collective-permute-start | bytes 196616 | tf_op jit(solution)/shard_map/ppermute | solution.py:59
  7.6 4.3 %collective-permute-start = (bf16[64,512]{1,0:T(8,128)(2,1)S(1)}, bf16[64,512]{1,0:T(8,128)(2,1)S(1)}, u32[]{:S(2)}, u32[]{:S(2)}) collective-permute-start(bf16[64,512]{1,0:T(8,128)(2,1)S(1)} %get-tuple-element.88), channel_id=1, source_target_pairs={{0,8},{1,9},{2,10},{3,11},{4,12},{5,13},{6,14},{7,15},{8,0},{9,1},... | collective-permute-start | bytes 196616 | tf_op jit(solution)/shard_map/ppermute | solution.py:59
  13.3 7.8 %collective-permute-start.3 = (bf16[192,512]{1,0:T(8,128)(2,1)S(1)}, bf16[192,512]{1,0:T(8,128)(2,1)S(1)}, u32[]{:S(2)}, u32[]{:S(2)}) collective-permute-start(bf16[192,512]{1,0:T(8,128)(2,1)S(1)} %get-tuple-element.78), channel_id=1, source_target_pairs={{0,4},{1,5},{2,6},{3,7},{4,0},{5,1},{6,2},{7,3},{8,12},{9,13},{10,... | collective-permute-start | bytes 589832 | tf_op jit(solution)/shard_map/ppermute | solution.py:59
  14.9 9.2 %collective-permute-start.5 = (bf16[128,512]{1,0:T(8,128)(2,1)S(1)}, bf16[128,512]{1,0:T(8,128)(2,1)S(1)}, u32[]{:S(2)}, u32[]{:S(2)}) collective-permute-start(bf16[128,512]{1,0:T(8,128)(2,1)S(1)} %pad_maximum_fusion), channel_id=1, source_target_pairs={{0,6},{1,7},{2,4},{3,5},{4,2},{5,3},{6,0},{7,1},{8,14},{9,15},{10,... | collective-permute-start | bytes 393224 | tf_op jit(solution)/shard_map/ppermute | solution.py:59
  16.4 7.6 %collective-permute-start.4 = (bf16[128,512]{1,0:T(8,128)(2,1)S(1)}, bf16[128,512]{1,0:T(8,128)(2,1)S(1)}, u32[]{:S(2)}, u32[]{:S(2)}) collective-permute-start(bf16[128,512]{1,0:T(8,128)(2,1)S(1)} %pad_maximum_fusion), channel_id=1, source_target_pairs={{0,2},{1,3},{2,0},{3,1},{4,6},{5,7},{6,4},{7,5},{8,10},{9,11},{10,... | collective-permute-start | bytes 393224 | tf_op jit(solution)/shard_map/ppermute | solution.py:59
  24.1 6.0 %collective-permute-start.6 = (bf16[512,512]{1,0:T(8,128)(2,1)S(1)}, bf16[512,512]{1,0:T(8,128)(2,1)S(1)}, u32[]{:S(2)}, u32[]{:S(2)}) collective-permute-start(bf16[512,512]{1,0:T(8,128)(2,1)S(1)} %constant_dynamic-update-slice_fusion.13.lo_ref), channel_id=1, source_target_pairs={{0,1},{1,0},{2,3},{3,2},{4,5},{5,4},{6,7},{7,6},{8,9},{9,8},{10,11... | collective-permute-start | bytes 1572872 | tf_op jit(solution)/shard_map/ppermute | solution.py:59
  34.8 2.5 %copy-start.6 = (bf16[128,512]{1,0:T(8,128)(2,1)S(1)}, bf16[128,512]{1,0:T(8,128)(2,1)}, u32[]{:S(2)}) copy-start(bf16[128,512]{1,0:T(8,128)(2,1)} %rim_ref.1) | copy-start | bytes 393220
  40.1 5.1 %collective-permute-start.7 = (bf16[512,512]{1,0:T(8,128)(2,1)S(1)}, bf16[512,512]{1,0:T(8,128)(2,1)S(1)}, u32[]{:S(2)}, u32[]{:S(2)}) collective-permute-start(bf16[512,512]{1,0:T(8,128)(2,1)S(1)} %get-tuple-element.32), channel_id=1, source_target_pairs={{0,1},{1,0},{2,3},{3,2},{4,5},{5,4},{6,7},{7,6},{8,9},{9,8},{10,11... | collective-permute-start | bytes 1572872 | tf_op jit(solution)/shard_map/ppermute | solution.py:59
  40.7 20.9 %copy-start.7 = (f32[2,16,512]{2,1,0:T(8,128)S(1)}, f32[2,16,512]{2,1,0:T(8,128)}, u32[]{:S(2)}) copy-start(f32[2,16,512]{2,1,0:T(8,128)} %master_hbm.1) | copy-start | bytes 196612
  40.7 20.9 %copy-start.8 = (f32[2,16,512]{2,1,0:T(8,128)S(1)}, f32[2,16,512]{2,1,0:T(8,128)}, u32[]{:S(2)}) copy-start(f32[2,16,512]{2,1,0:T(8,128)} %param.19) | copy-start | bytes 196612
  40.7 20.9 %copy-start.9 = (f32[2,16,512]{2,1,0:T(8,128)S(1)}, f32[2,16,512]{2,1,0:T(8,128)}, u32[]{:S(2)}) copy-start(f32[2,16,512]{2,1,0:T(8,128)} %param.18) | copy-start | bytes 196612
  40.7 6.6 %collective-permute-start.20 = (bf16[64,512]{1,0:T(8,128)(2,1)S(1)}, bf16[64,512]{1,0:T(8,128)(2,1)S(1)}, u32[]{:S(2)}, u32[]{:S(2)}) collective-permute-start(bf16[64,512]{1,0:T(8,128)(2,1)S(1)} %pad_maximum_fusion.6), channel_id=1, source_target_pairs={{0,8},{1,9},{2,10},{3,11},{4,12},{5,13},{6,14},{7,15},{8,0},{9,1},... | collective-permute-start | bytes 196616 | tf_op jit(solution)/shard_map/ppermute | solution.py:59
  40.8 17.1 %collective-permute-start.21 = (bf16[64,512]{1,0:T(8,128)(2,1)S(1)}, bf16[64,512]{1,0:T(8,128)(2,1)S(1)}, u32[]{:S(2)}, u32[]{:S(2)}) collective-permute-start(bf16[64,512]{1,0:T(8,128)(2,1)S(1)} %pad_maximum_fusion.7), channel_id=1, source_target_pairs={{0,16},{1,17},{2,18},{3,19},{4,20},{5,21},{6,22},{7,23},{8,24},{9,... | collective-permute-start | bytes 196616 | tf_op jit(solution)/shard_map/ppermute | solution.py:59
  42.9 33.9 %collective-permute-start.22 = (bf16[64,512]{1,0:T(8,128)(2,1)S(1)}, bf16[64,512]{1,0:T(8,128)(2,1)S(1)}, u32[]{:S(2)}, u32[]{:S(2)}) collective-permute-start(bf16[64,512]{1,0:T(8,128)(2,1)S(1)} %pad_maximum_fusion.8), channel_id=1, source_target_pairs={{0,24},{1,25},{2,26},{3,27},{4,28},{5,29},{6,30},{7,31},{8,16},{9,... | collective-permute-start | bytes 196616 | tf_op jit(solution)/shard_map/ppermute | solution.py:59
  45.4 6.1 %collective-permute-start.8 = (bf16[128,512]{1,0:T(8,128)(2,1)S(1)}, bf16[128,512]{1,0:T(8,128)(2,1)S(1)}, u32[]{:S(2)}, u32[]{:S(2)}) collective-permute-start(bf16[128,512]{1,0:T(8,128)(2,1)S(1)} %get-tuple-element.39), channel_id=1, source_target_pairs={{0,4},{1,5},{2,6},{3,7},{4,0},{5,1},{6,2},{7,3},{8,12},{9,13},{10,... | collective-permute-start | bytes 393224 | tf_op jit(solution)/shard_map/ppermute | solution.py:59
  46.9 6.2 %collective-permute-start.10 = (bf16[128,512]{1,0:T(8,128)(2,1)S(1)}, bf16[128,512]{1,0:T(8,128)(2,1)S(1)}, u32[]{:S(2)}, u32[]{:S(2)}) collective-permute-start(bf16[128,512]{1,0:T(8,128)(2,1)S(1)} %get-tuple-element.40), channel_id=1, source_target_pairs={{0,6},{1,7},{2,4},{3,5},{4,2},{5,3},{6,0},{7,1},{8,14},{9,15},{10,... | collective-permute-start | bytes 393224 | tf_op jit(solution)/shard_map/ppermute | solution.py:59
  47.3 7.0 %collective-permute-start.9 = (bf16[128,512]{1,0:T(8,128)(2,1)S(1)}, bf16[128,512]{1,0:T(8,128)(2,1)S(1)}, u32[]{:S(2)}, u32[]{:S(2)}) collective-permute-start(bf16[128,512]{1,0:T(8,128)(2,1)S(1)} %get-tuple-element.41), channel_id=1, source_target_pairs={{0,2},{1,3},{2,0},{3,1},{4,6},{5,7},{6,4},{7,5},{8,10},{9,11},{10,... | collective-permute-start | bytes 393224 | tf_op jit(solution)/shard_map/ppermute | solution.py:59
  54.4 4.0 %collective-permute-start.11 = (bf16[32,512]{1,0:T(8,128)(2,1)S(1)}, bf16[32,512]{1,0:T(8,128)(2,1)S(1)}, u32[]{:S(2)}, u32[]{:S(2)}) collective-permute-start(bf16[32,512]{1,0:T(8,128)(2,1)S(1)} %get-tuple-element.52), channel_id=1, source_target_pairs={{0,8},{1,9},{2,10},{3,11},{4,12},{5,13},{6,14},{7,15},{8,0},{9,1},... | collective-permute-start | bytes 98312 | tf_op jit(solution)/shard_map/ppermute | solution.py:59
  54.5 5.8 %collective-permute-start.13 = (bf16[32,512]{1,0:T(8,128)(2,1)S(1)}, bf16[32,512]{1,0:T(8,128)(2,1)S(1)}, u32[]{:S(2)}, u32[]{:S(2)}) collective-permute-start(bf16[32,512]{1,0:T(8,128)(2,1)S(1)} %get-tuple-element.53), channel_id=1, source_target_pairs={{0,24},{1,25},{2,26},{3,27},{4,28},{5,29},{6,30},{7,31},{8,16},{9,... | collective-permute-start | bytes 98312 | tf_op jit(solution)/shard_map/ppermute | solution.py:59
  56.7 4.8 %collective-permute-start.12 = (bf16[32,512]{1,0:T(8,128)(2,1)S(1)}, bf16[32,512]{1,0:T(8,128)(2,1)S(1)}, u32[]{:S(2)}, u32[]{:S(2)}) collective-permute-start(bf16[32,512]{1,0:T(8,128)(2,1)S(1)} %get-tuple-element.54), channel_id=1, source_target_pairs={{0,16},{1,17},{2,18},{3,19},{4,20},{5,21},{6,22},{7,23},{8,24},{9,... | collective-permute-start | bytes 98312 | tf_op jit(solution)/shard_map/ppermute | solution.py:59
  62.3 5.7 %collective-permute-start.16 = (bf16[32,512]{1,0:T(8,128)(2,1)S(1)}, bf16[32,512]{1,0:T(8,128)(2,1)S(1)}, u32[]{:S(2)}, u32[]{:S(2)}) collective-permute-start(bf16[32,512]{1,0:T(8,128)(2,1)S(1)} %bitcast.10), channel_id=1, source_target_pairs={{0,24},{1,25},{2,26},{3,27},{4,28},{5,29},{6,30},{7,31},{8,16},{9,... | collective-permute-start | bytes 98312 | tf_op jit(solution)/shard_map/ppermute | solution.py:59
  63.9 4.9 %collective-permute-start.15 = (bf16[32,512]{1,0:T(8,128)(2,1)S(1)}, bf16[32,512]{1,0:T(8,128)(2,1)S(1)}, u32[]{:S(2)}, u32[]{:S(2)}) collective-permute-start(bf16[32,512]{1,0:T(8,128)(2,1)S(1)} %bitcast.11), channel_id=1, source_target_pairs={{0,16},{1,17},{2,18},{3,19},{4,20},{5,21},{6,22},{7,23},{8,24},{9,... | collective-permute-start | bytes 98312 | tf_op jit(solution)/shard_map/ppermute | solution.py:59
  64.8 4.3 %collective-permute-start.14 = (bf16[32,512]{1,0:T(8,128)(2,1)S(1)}, bf16[32,512]{1,0:T(8,128)(2,1)S(1)}, u32[]{:S(2)}, u32[]{:S(2)}) collective-permute-start(bf16[32,512]{1,0:T(8,128)(2,1)S(1)} %bitcast.12), channel_id=1, source_target_pairs={{0,8},{1,9},{2,10},{3,11},{4,12},{5,13},{6,14},{7,15},{8,0},{9,1},... | collective-permute-start | bytes 98312 | tf_op jit(solution)/shard_map/ppermute | solution.py:59
  69.1 7.6 %collective-permute-start.19 = (bf16[128,512]{1,0:T(8,128)(2,1)S(1)}, bf16[128,512]{1,0:T(8,128)(2,1)S(1)}, u32[]{:S(2)}, u32[]{:S(2)}) collective-permute-start(bf16[128,512]{1,0:T(8,128)(2,1)S(1)} %pad_maximum_fusion.1), channel_id=1, source_target_pairs={{0,6},{1,7},{2,4},{3,5},{4,2},{5,3},{6,0},{7,1},{8,14},{9,15},{10,... | collective-permute-start | bytes 393224 | tf_op jit(solution)/shard_map/ppermute | solution.py:59
  71.1 5.5 %collective-permute-start.18 = (bf16[128,512]{1,0:T(8,128)(2,1)S(1)}, bf16[128,512]{1,0:T(8,128)(2,1)S(1)}, u32[]{:S(2)}, u32[]{:S(2)}) collective-permute-start(bf16[128,512]{1,0:T(8,128)(2,1)S(1)} %pad_maximum_fusion.1), channel_id=1, source_target_pairs={{0,2},{1,3},{2,0},{3,1},{4,6},{5,7},{6,4},{7,5},{8,10},{9,11},{10,... | collective-permute-start | bytes 393224 | tf_op jit(solution)/shard_map/ppermute | solution.py:59
  71.6 5.0 %collective-permute-start.17 = (bf16[128,512]{1,0:T(8,128)(2,1)S(1)}, bf16[128,512]{1,0:T(8,128)(2,1)S(1)}, u32[]{:S(2)}, u32[]{:S(2)}) collective-permute-start(bf16[128,512]{1,0:T(8,128)(2,1)S(1)} %pad_maximum_fusion.1), channel_id=1, source_target_pairs={{0,4},{1,5},{2,6},{3,7},{4,0},{5,1},{6,2},{7,3},{8,12},{9,13},{10,... | collective-permute-start | bytes 393224 | tf_op jit(solution)/shard_map/ppermute | solution.py:59
  76.7 7.4 %collective-permute-start.24 = (bf16[512,512]{1,0:T(8,128)(2,1)S(1)}, bf16[512,512]{1,0:T(8,128)(2,1)S(1)}, u32[]{:S(2)}, u32[]{:S(2)}) collective-permute-start(bf16[512,512]{1,0:T(8,128)(2,1)S(1)} %constant_dynamic-update-slice_fusion.19.part_ref), channel_id=1, source_target_pairs={{0,1},{1,0},{2,3},{3,2},{4,5},{5,4},{6,7},{7,6},{8,9},{9,8},{10,11... | collective-permute-start | bytes 1572872 | tf_op jit(solution)/shard_map/ppermute | solution.py:59
  76.8 6.0 %collective-permute-start.23 = (bf16[128,512]{1,0:T(8,128)(2,1)S(1)}, bf16[128,512]{1,0:T(8,128)(2,1)S(1)}, u32[]{:S(2)}, u32[]{:S(2)}) collective-permute-start(bf16[128,512]{1,0:T(8,128)(2,1)S(1)} %pad_maximum_fusion.2), channel_id=1, source_target_pairs={{0,4},{1,5},{2,6},{3,7},{4,0},{5,1},{6,2},{7,3},{8,12},{9,13},{10,... | collective-permute-start | bytes 393224 | tf_op jit(solution)/shard_map/ppermute | solution.py:59
  (3 other events, 6.6 us)
where the time goes:
time: 85.4 us; the launch traced here: 85.2 us
  starting transfers between devices  30.6 us (36%)
  waiting for transfers between devices  30.5 us (36%)
  Pallas kernels  21.6 us (25%)
  between operations  1.12 us (1%)
  other arithmetic  0.99 us (1%)
    ppermute x25, starting transfers between devices, swap(): return lax.ppermute(x, AXES, pairs)  30.6 us
    ppermute x25, waiting for transfers between devices, swap(): return lax.ppermute(x, AXES, pairs)  30.5 us
    pallas_call x1, Pallas kernels, epoch(): call(part(spread_kernel, lay), sds((local + rim, width), F32), [SMEM, SME...  4.6 us
    pallas_call x1, Pallas kernels, epoch(): call(prepare_kernel, (sds((blocks * tiles + 1, edge, edge), BF16), sds((l...  3.7 us
    pallas_call x1, Pallas kernels, epoch(): call(part(second_kernel, lay), (nodes, grads_half, grads_half), [SMEM, VM...  2.81 us
    pallas_call x1, Pallas kernels, epoch(): call(part(hidden_kernel, lay), (nodes, sds((2 * rim, width), BF16), squar...  2.49 us
    pallas_call x1, Pallas kernels, epoch(): call(part(first_kernel, lay), (nodes, sds((width, local), BF16)), [SMEM,...  2.13 us
    pallas_call x1, Pallas kernels, epoch(): call(part(out_kernel, lay), nodes, [VMEM, VMEM, VMEM], VMEM, [pltpu.VMEM(...  1.77 us
  transfers between devices with their start and end apart: 25, of which 15 were waited for; matrix products, arithmetic and copies ran while one was open for 1% of the time, Pallas kernels for 10%

commit v1 on v0

--- a/solution.py
+++ b/solution.py
@@ -27,7 +27,7 @@
 PACK = 16
 LAYERS = 2
 GROUP = 4
-BATCH = 5
+STRIP = 256
 
 
 def plan_stages(nd, ng):
@@ -78,15 +78,14 @@
 
 
 def reduce_relative(keep, send, stages):
-    got = swap(send, stages[0][1])
-    total = keep.astype(F32) + got.astype(F32)
-    for members in stages[1:]:
-        pieces = jnp.split(total.astype(BF16), len(members), 0)
-        got = [swap(p, m) for p, m in zip(pieces[1:], members[1:])]
-        total = pieces[0].astype(F32)
-        for g in got:
-            total = total + g.astype(F32)
-    return total
+    pieces = []
+    for k, s in zip(*(jnp.split(x, len(stages[1]), 0) for x in (keep, send))):
+        pieces.append((k.astype(F32) + swap(s, stages[0][1]).astype(F32)).astype(BF16))
+    for n, members in enumerate(stages[1:]):
+        if n:
+            pieces = jnp.split(sum(t.astype(F32) for t in terms).astype(BF16), len(members), 0)
+        terms = [pieces[0]] + [swap(p, m) for p, m in zip(pieces[1:], members[1:])]
+    return terms
 
 
 def dom_stages(stages):
@@ -132,6 +131,10 @@
 
 def rows(start, size):
     return pl.ds(pl.multiple_of(start * size, size), size)
+
+
+def strips(width):
+    return [slice(n, n + STRIP) for n in range(0, width, STRIP)]
 
 
 def begin_kernel(lay, sel_hbm, master_hbm, rows_ref, own_ref, out_ref, sel_ref, master_ref, sems):
@@ -154,18 +157,15 @@
         c.wait()
 
 
-def prepare_kernel(src_ref, tile_ref, turned_ref, list_ref, goal_ref, count_ref):
+def prepare_kernel(src_ref, tile_hbm, turned_ref, list_ref, goal_ref, bound_ref, tile_ref, count_ref, sems):
     blocks, tiles = tile_ref.shape[:2]
+    copies = [pltpu.make_async_copy(tile_hbm.at[i], tile_ref.at[i], sems.at[i]) for i in range(blocks)]
+    for c in copies:
+        c.start()
     total = blocks * tiles
     slots = count_ref.shape[0]
     groups = goal_ref.shape[0]
 
-    def turn(i, carry):
-        for t in range(tiles):
-            turned_ref[i * tiles + t] = tile_ref[i, t].T
-        return carry
-
-    lax.fori_loop(0, blocks, turn, 0)
     turned_ref[total] = jnp.zeros_like(turned_ref[total])
     for b in range(slots):
         count_ref[b] = 0
@@ -193,6 +193,8 @@
 
         lax.fori_loop(first, first + need, mark, 0)
         count_ref[b] = first * GROUP
+        if b == blocks:
+            bound_ref[0] = first * GROUP
         first = first + need
 
     def rest(g, carry):
@@ -200,7 +202,7 @@
         return carry
 
     lax.fori_loop(first, groups, rest, 0)
-    goal_ref[groups - 1] = first
+    bound_ref[1] = first * GROUP
 
     def enter(i, carry):
         for t in range(tiles):
@@ -211,6 +213,10 @@
         return carry
 
     lax.fori_loop(0, blocks, enter, 0)
+    for i in range(blocks):
+        copies[i].wait()
+        for t in range(tiles):
+            turned_ref[i * tiles + t] = tile_ref[i, t].T
 
 
 def aggregate_block(i, src_ref, tile_ref, table_ref):
@@ -259,44 +265,33 @@
     piece = stale_ref.shape[0] // peers
     assemble(lay, w_ref, (lo_ref, hi_ref), 1)
     acc_ref[...] = jnp.zeros_like(acc_ref)
-    for i in range(blocks):
-        at = slice(i * edge, (i + 1) * edge)
-        up_ref[at, :] = dot(og_ref[at, :], w_ref[...], 1, 1).astype(BF16)
-
-    def body(n, carry):
-        sums = []
-        for u in range(BATCH):
-            g = n * BATCH + u
-            ks = [list_ref[g * GROUP + j] for j in range(GROUP)]
-            left = jnp.concatenate([turned_ref[k] for k in ks], 1)
-            right = jnp.concatenate([up_ref[rows(jnp.minimum(k // tiles, blocks - 1), edge), :] for k in ks], 0)
-            sums.append((rows(goal_ref[g], edge), dot(left, right)))
-        for at, part in sums:
-            acc_ref[at, :] += part
-        return carry
-
-    used = goal_ref[goal_ref.shape[0] - 1]
-    lax.fori_loop(0, (used + (BATCH - 1)) // BATCH, body, 0)
+    for n in strips(w_ref.shape[0]):
+        up_ref[:, n] = dot(og_ref[...], w_ref[n, :], 1, 1).astype(BF16)
+
+    for g in range(goal_ref.shape[0]):
+        ks = [list_ref[g * GROUP + j] for j in range(GROUP)]
+        left = jnp.concatenate([turned_ref[k] for k in ks], 1)
+        right = jnp.concatenate([up_ref[rows(jnp.minimum(k // tiles, blocks - 1), edge), :] for k in ks], 0)
+        acc_ref[rows(goal_ref[g], edge), :] += dot(left, right)
     for p in range(peers):
         at = rows(sel_ref[p], piece)
         acc_ref[at, :] += stale_ref[p * piece : (p + 1) * piece, :].astype(F32)
 
 
-def hidden_kernel(lay, sel_ref, p_ref, turned_ref, acc_ref, lo_ref, hi_ref, h_ref, route_ref, full_ref, w_ref, dz_ref):
-    step = 128
+def hidden_kernel(
+    lay, sel_ref, p_ref, turned_ref, acc_ref, rim_ref, lo_ref, hi_ref, h_ref, route_ref, full_ref, w_ref, dz_ref
+):
     local = p_ref.shape[0]
+    h_ref[local:, :] = rim_ref[...]
     peers = len(lay.peers)
     piece = (acc_ref.shape[0] - local) // peers
     assemble(lay, w_ref, (lo_ref, hi_ref), 0)
-    for i in range(local // step):
-        at = slice(i * step, (i + 1) * step)
-        z = dot(p_ref[at, :], w_ref[...])
+    for n in strips(w_ref.shape[1]):
+        z = dot(p_ref[...], w_ref[:, n])
         s = 1.0 / (1.0 + jnp.exp(-z))
-        h_ref[at, :] = (z * s).astype(BF16)
-        dz_ref[at, :] = (acc_ref[at, :] * s * (1.0 + z * (1.0 - s))).astype(BF16)
-    for m in range(full_ref.shape[0] // step):
-        at = slice(m * step, (m + 1) * step)
-        full_ref[at, :] = dot(turned_ref[at, :], dz_ref[...])
+        h_ref[:local, n] = (z * s).astype(BF16)
+        dz_ref[:, n] = (acc_ref[:local, n] * s * (1.0 + z * (1.0 - s))).astype(BF16)
+        full_ref[:, n] = dot(turned_ref[...], dz_ref[:, n])
     for r in range(peers):
         q = lay.peer(r)
         at = 2 * r * piece
@@ -305,27 +300,48 @@
         route_ref[at + piece : at + 2 * piece, :] = back.astype(BF16)
 
 
-def second_kernel(lay, src_ref, h_ref, rim_ref, tile_ref, og_ref, first_ref, p_ref, keep_ref, send_ref, table_ref, full_ref):
+def second_kernel(lay, src_ref, table_ref, tile_ref, og_ref, first_ref, p_ref, keep_ref, send_ref, full_ref):
     blocks, edge = tile_ref.shape[0], tile_ref.shape[2]
-    step = 128
-    local = h_ref.shape[0]
-    table_ref[:local, :] = h_ref[...]
-    table_ref[local:, :] = rim_ref[...]
     for i in range(blocks):
         p_ref[i * edge : (i + 1) * edge, :] = aggregate_block(i, src_ref, tile_ref, table_ref)
-    for m in range(full_ref.shape[0] // step):
-        cols = slice(m * step, (m + 1) * step)
-        full_ref[cols, :] = dot(p_ref[:, cols], og_ref[...], 0, 0)
+    for n in strips(full_ref.shape[1]):
+        full_ref[:, n] = dot(p_ref[...], og_ref[:, n], 0, 0)
     scatter_grad(lay, first_ref, (keep_ref, send_ref), 0)
     scatter_grad(lay, full_ref, (keep_ref, send_ref), 1)
 
 
 def out_kernel(lay, p_ref, lo_ref, hi_ref, out_ref, w_ref):
-    step = 128
     assemble(lay, w_ref, (lo_ref, hi_ref), 1)
-    for i in range(p_ref.shape[0] // step):
-        at = slice(i * step, (i + 1) * step)
-        out_ref[at, :] = dot(p_ref[at, :], w_ref[...]).astype(BF16)
+    for n in strips(w_ref.shape[1]):
+        out_ref[:, n] = dot(p_ref[...], w_ref[:, n]).astype(BF16)
+
+
+def adam_step(total_nodes, layer, parts, master_ref, first_ref, second_ref):
+    shard_rows = master_ref.shape[1]
+    at = slice(layer * shard_rows, (layer + 1) * shard_rows)
+    shard = parts[0][at, :].astype(F32)
+    for p in parts[1:]:
+        shard = shard + p[at, :].astype(F32)
+    shard = shard / total_nodes
+    moment_new = decay_first * first_ref[layer] + (1.0 - decay_first) * shard
+    second_new = decay_second * second_ref[layer] + (1.0 - decay_second) * shard * shard
+    update = (
+        moment_new
+        / (1.0 - decay_first**STEP)
+        / (jnp.sqrt(second_new / (1.0 - decay_second**STEP)) + epsilon)
+    )
+    return at, master_ref[layer] - learn_rate * update
+
+
+def adam_kernel(total_nodes, *refs):
+    for layer in range(LAYERS):
+        at, after = adam_step(total_nodes, layer, refs[:-4], *refs[-4:-1])
+        refs[-1][at, :] = after.astype(BF16)
+
+
+def settle_kernel(total_nodes, *refs):
+    for layer in range(LAYERS):
+        refs[-1][layer] = adam_step(total_nodes, layer, refs[:-4], *refs[-4:-1])[1]
 
 
 def place_rows(lay, half_at, part_ref, out_ref):
@@ -429,8 +445,7 @@
     nodes = sds((local, width), BF16)
     square = sds((full_rows, width), F32)
     grads_half = sds((half, width), BF16)
-    listed = -(-(blocks * tiles + slots * (GROUP - 1)) // GROUP)
-    listed = -(-listed // BATCH) * BATCH + 1
+    listed = (blocks * tiles + slots * (GROUP - 1)) // GROUP
     part = functools.partial
 
     own, picked = call(
@@ -451,19 +466,24 @@
     )
     lo, hi = spread_out(lo, hi)
     raw_rim = jnp.concatenate(raw_rim, 0)
-    turned_tiles, order, goal = call(
+    turned_tiles, order, goal, _ = call(
         prepare_kernel,
         (
             sds((blocks * tiles + 1, edge, edge), BF16),
             sds((listed * GROUP,), jnp.int32),
             sds((listed,), jnp.int32),
+            sds((2,), jnp.int32),
         ),
-        [SMEM, VMEM],
-        (VMEM, SMEM, SMEM),
-        [pltpu.SMEM((slots,), jnp.int32)],
+        [SMEM, HBM],
+        (VMEM, SMEM, SMEM, SMEM),
+        [
+            pltpu.VMEM(tile_val.shape, BF16),
+            pltpu.SMEM((slots,), jnp.int32),
+            pltpu.SemaphoreType.DMA((blocks,)),
+        ],
         0,
         2 * tile_bytes,
-    )(tile_src, tile_val)
+    )(tile_src, pltpu.with_memory_space_constraint(tile_val, pltpu.HBM))
     p_first, p_turned = call(
         part(first_kernel, lay),
         (nodes, sds((width, local), BF16)),
@@ -482,25 +502,25 @@
         tile_flops + dense_flops,
         tile_bytes + 3 * node_bytes,
     )(order, goal, selects, out_grad, turned_tiles, lo, hi, stale_grads)
-    h_first, route, g_first = call(
+    sources, route, g_first = call(
         part(hidden_kernel, lay),
-        (nodes, sds((2 * rim, width), BF16), square),
-        [SMEM, VMEM, VMEM, VMEM, VMEM, VMEM],
+        (sds((local + rim, width), BF16), sds((2 * rim, width), BF16), square),
+        [SMEM, VMEM, VMEM, VMEM, VMEM, VMEM, VMEM],
         (VMEM, VMEM, VMEM),
         [pltpu.VMEM((full_rows, width), BF16), pltpu.VMEM((local, width), BF16)],
         2 * dense_flops,
         4 * node_bytes,
-    )(selects, p_first, p_turned, acc, lo, hi)
+    )(selects, p_first, p_turned, acc, stale_features, lo, hi)
     p_second, keep, send = call(
         part(second_kernel, lay),
         (nodes, grads_half, grads_half),
-        [SMEM, VMEM, VMEM, VMEM, VMEM, VMEM],
+        [SMEM, VMEM, VMEM, VMEM, VMEM],
         (VMEM, VMEM, VMEM),
-        [pltpu.VMEM((local + rim, width), BF16), pltpu.VMEM((full_rows, width), F32)],
+        [pltpu.VMEM((full_rows, width), F32)],
         tile_flops + dense_flops,
         tile_bytes + 3 * node_bytes,
-    )(tile_src, h_first, stale_features, tile_val, out_grad, g_first)
-    shard = reduce_relative(*draw_in(keep, send), lay.stages).reshape(layers, shard_rows, width) / total_nodes
+    )(tile_src, sources, tile_val, out_grad, g_first)
+    total = reduce_relative(*draw_in(keep, send), lay.stages)
     layer_out = call(
         part(out_kernel, lay),
         nodes,
@@ -512,11 +532,19 @@
     )(p_second, lo, hi)
     fresh = jnp.concatenate(exchange(jnp.split(route, peers, 0), lay.ways, range(len(lay.ways))[::-1]), 0)
 
-    moment_new = decay_first * moment_first + (1.0 - decay_first) * shard
-    second_new = decay_second * moment_second + (1.0 - decay_second) * shard * shard
-    update = moment_new / (1.0 - decay_first**STEP) / (jnp.sqrt(second_new / (1.0 - decay_second**STEP)) + epsilon)
-    master_next = master - learn_rate * update
-    moved = master_next.astype(BF16).reshape(layers * shard_rows, width)
+    state = (*total, master, moment_first, moment_second)
+    moved = call(
+        part(adam_kernel, total_nodes),
+        sds((layers * shard_rows, width), BF16),
+        [VMEM] * len(state),
+        VMEM,
+        [],
+        0,
+        12 * master.size,
+    )(*state)
+    master_next = call(
+        part(settle_kernel, total_nodes), sds(master.shape, F32), [VMEM] * len(state), VMEM, [], 0, 12 * master.size
+    )(*state)
     lo_next, hi_next, _ = gather_relative(moved, lay.stages)
     lo_next, hi_next = spread_out(lo_next, hi_next)
     weights = sds((layers, full_rows, width), BF16)

time: 85.4 us -> 84.2 us (0.986)
  starting transfers between devices: 30.6 us -> 32 us
  waiting for transfers between devices: 30.5 us -> 29.2 us
    ppermute x25 -> x28, starting transfers between devices: 30.6 us -> 32 us  [swap(): return lax.ppermute(x, AXES, pairs)]
    ppermute x25 -> x28, waiting for transfers between devices: 30.5 us -> 29.2 us  [swap(): return lax.ppermute(x, AXES, pairs)]
    pallas_call x1, Pallas kernels: 4.6 us -> 3.54 us  [epoch(): call(part(spread_kernel, lay), sds((local + rim, width), F32), [SMEM, SME...]
    pallas_call x1 -> x3, Pallas kernels: 2.49 us -> 3.4 us  [the longest x1 2.61 us: epoch(): call(part(hidden_kernel, lay), (sds((local + rim, width), BF16), sds((2 *...]
  transfers between devices with their start and end apart: 25 -> 28, of which waited for: 15 -> 13; matrix products, arithmetic and copies ran while one was open for 1% -> 0% of each run, Pallas kernels for 10% -> 14%
where the time goes in v1:
time: 84.2 us; the launch traced here: 83.9 us
  starting transfers between devices  32 us (38%)
  waiting for transfers between devices  29.2 us (35%)
  Pallas kernels  21.1 us (25%)
  between operations  1.12 us (1%)
    ppermute x28, starting transfers between devices, swap(): return lax.ppermute(x, AXES, pairs)  32 us
    ppermute x28, waiting for transfers between devices, swap(): return lax.ppermute(x, AXES, pairs)  29.2 us
    pallas_call x1, Pallas kernels, epoch(): call(prepare_kernel, (sds((blocks * tiles + 1, edge, edge), BF16), sds((l...  3.56 us
    pallas_call x1, Pallas kernels, epoch(): call(part(spread_kernel, lay), sds((local + rim, width), F32), [SMEM, SME...  3.54 us
    pallas_call x1, Pallas kernels, epoch(): call(part(hidden_kernel, lay), (sds((local + rim, width), BF16), sds((2 *...  2.61 us
    pallas_call x1, Pallas kernels, epoch(): call(part(second_kernel, lay), (nodes, grads_half, grads_half), [SMEM, VM...  2.6 us
    pallas_call x1, Pallas kernels, epoch(): call(part(first_kernel, lay), (nodes, sds((width, local), BF16)), [SMEM,...  2.13 us
    pallas_call x1, Pallas kernels, epoch(): call(part(out_kernel, lay), nodes, [VMEM, VMEM, VMEM], VMEM, [pltpu.VMEM(...  1.74 us
  transfers between devices with their start and end apart: 28, of which 13 were waited for; matrix products, arithmetic and copies ran while one was open for 0% of the time, Pallas kernels for 14%

profile of v1, /device:TPU:0, one launch (start us, length us, event | category | flops | bytes accessed | tf_op | source)
XLA Modules:
  0.0 83.9 jit_solution(14439106050177795073)
XLA Ops:
  0.6 1.7 %shard_map.137 = (bf16[2,16,512]{2,1,0:T(8,128)(2,1)S(1)}, bf16[128,512]{1,0:T(8,128)(2,1)S(1)}) custom-call(s32[1,8]{1,0:T(1,128)} %sel_hbm.1, f32[2,16,512]{2,1,0:T(8,128)} %refs_4_.3, bf16[1024,512]{1,0:T(8,128)(2,1)} %feat_ref.1), custom_call_target="tpu_custom_call" | custom-call | bytes 262144 | tf_op jit(solution)/shard_map/pallas_call | solution.py:451
  2.5 5.1 %collective-permute-start.2 = (bf16[64,512]{1,0:T(8,128)(2,1)S(1)}, bf16[64,512]{1,0:T(8,128)(2,1)S(1)}, u32[]{:S(2)}, u32[]{:S(2)}) collective-permute-start(bf16[64,512]{1,0:T(8,128)(2,1)S(1)} %get-tuple-element.87), channel_id=1, source_target_pairs={{0,24},{1,25},{2,26},{3,27},{4,28},{5,29},{6,30},{7,31},{8,16},{9,... | collective-permute-start | bytes 196616 | tf_op jit(solution)/shard_map/ppermute | solution.py:59
  8.2 3.6 %collective-permute-done = bf16[64,512]{1,0:T(8,128)(2,1)S(1)} collective-permute-done((bf16[64,512]{1,0:T(8,128)(2,1)S(1)}, bf16[64,512]{1,0:T(8,128)(2,1)S(1)}, u32[]{:S(2)}, u32[]{:S(2)}) %collective-permute-start) | collective-permute-done | bytes 65568 | tf_op jit(solution)/shard_map/ppermute | solution.py:59
  11.9 1.3 %collective-permute-done.1 = bf16[64,512]{1,0:T(8,128)(2,1)S(1)} collective-permute-done((bf16[64,512]{1,0:T(8,128)(2,1)S(1)}, bf16[64,512]{1,0:T(8,128)(2,1)S(1)}, u32[]{:S(2)}, u32[]{:S(2)}) %collective-permute-start.1) | collective-permute-done | bytes 65568 | tf_op jit(solution)/shard_map/ppermute | solution.py:59
  13.3 1.6 %collective-permute-start.3 = (bf16[192,512]{1,0:T(8,128)(2,1)S(1)}, bf16[192,512]{1,0:T(8,128)(2,1)S(1)}, u32[]{:S(2)}, u32[]{:S(2)}) collective-permute-start(bf16[192,512]{1,0:T(8,128)(2,1)S(1)} %get-tuple-element.79), channel_id=1, source_target_pairs={{0,4},{1,5},{2,6},{3,7},{4,0},{5,1},{6,2},{7,3},{8,12},{9,13},{10,... | collective-permute-start | bytes 589832 | tf_op jit(solution)/shard_map/ppermute | solution.py:59
  14.9 1.6 %collective-permute-start.5 = (bf16[128,512]{1,0:T(8,128)(2,1)S(1)}, bf16[128,512]{1,0:T(8,128)(2,1)S(1)}, u32[]{:S(2)}, u32[]{:S(2)}) collective-permute-start(bf16[128,512]{1,0:T(8,128)(2,1)S(1)} %pad_maximum_fusion), channel_id=1, source_target_pairs={{0,6},{1,7},{2,4},{3,5},{4,2},{5,3},{6,0},{7,1},{8,14},{9,15},{10,... | collective-permute-start | bytes 393224 | tf_op jit(solution)/shard_map/ppermute | solution.py:59
  16.9 4.2 %collective-permute-done.3 = bf16[192,512]{1,0:T(8,128)(2,1)S(1)} collective-permute-done((bf16[192,512]{1,0:T(8,128)(2,1)S(1)}, bf16[192,512]{1,0:T(8,128)(2,1)S(1)}, u32[]{:S(2)}, u32[]{:S(2)}) %collective-permute-start.3) | collective-permute-done | bytes 196640 | tf_op jit(solution)/shard_map/ppermute | solution.py:59
  21.1 2.9 %collective-permute-done.4 = bf16[128,512]{1,0:T(8,128)(2,1)S(1)} collective-permute-done((bf16[128,512]{1,0:T(8,128)(2,1)S(1)}, bf16[128,512]{1,0:T(8,128)(2,1)S(1)}, u32[]{:S(2)}, u32[]{:S(2)}) %collective-permute-start.4) | collective-permute-done | bytes 131104 | tf_op jit(solution)/shard_map/ppermute | solution.py:59
  24.2 3.6 %shard_map.139 = (bf16[65,128,128]{2,1,0:T(8,128)(2,1)S(1)}, s32[88]{0:T(128)S(1)}, s32[22]{0:T(128)S(1)}, s32[2]{0:T(128)}) custom-call(s32[8,8]{1,0:T(8,128)S(1)} %copy-done.9, bf16[8,8,128,128]{3,2,1,0:T(8,128)(2,1)} %tile_ref.3), custom_call_target="tpu_custom_call" | custom-call | bytes 4194304 | tf_op jit(solution)/shard_map/pallas_call | solution.py:469
  27.8 2.1 %shard_map.138 = (bf16[1024,512]{1,0:T(8,128)(2,1)S(1)}, bf16[512,1024]{1,0:T(8,128)(2,1)S(1)}) custom-call(s32[8,8]{1,0:T(8,128)S(1)} %copy-done.9, bf16[1024,512]{1,0:T(8,128)(2,1)S(1)} %copy-done.1, bf16[128,512]{1,0:T(8,128)(2,1)S(1)} %constant_dynamic-update-slice_fusion.8.rim_ref, bf16[8,8,128,128]{3,2,1,0:T(8,128)(2,1)S(1)} %copy-done), custom_call_target="tpu_custom_call" | custom-call | flops 1073741824 | bytes 4194304 | tf_op jit(solution)/shard_map/pallas_call | solution.py:487
  30.0 3.5 %shard_map.140.acc_ref = f32[1152,512]{1,0:T(8,128)S(1)} custom-call(s32[88]{0:T(128)S(1)} %get-tuple-element.25.list_ref, s32[22]{0:T(128)S(1)} %get-tuple-element.26.goal_ref, s32[8]{0:T(128)S(1)} %bitcast.5, bf16[1024,512]{1,0:T(8,128)(2,1)S(1)} %copy-done.2, bf16[65,128,128]{2,1,0:T(8,128)(2,1)S(1)} %get-tuple-element.27.turned_ref, ...), custom_call_target="tpu_custom_call" | custom-call | flops 1610612736 | bytes 5242880 | tf_op jit(solution)/shard_map/pallas_call | solution.py:496
  33.6 2.6 %shard_map.141 = (bf16[1152,512]{1,0:T(8,128)(2,1)S(1)}, bf16[256,512]{1,0:T(8,128)(2,1)S(1)}, f32[512,512]{1,0:T(8,128)S(1)}) custom-call(s32[8]{0:T(128)S(1)} %bitcast.6, bf16[1024,512]{1,0:T(8,128)(2,1)S(1)} %get-tuple-element.23.p_ref, bf16[512,1024]{1,0:T(8,128)(2,1)S(1)} %get-tuple-element.24.turned_ref, f32[1152,512]{1,0:T(8,128)S(1)} %shard_map.140.acc_ref, ...), custom_call_target="tpu_custom_call" | custom-call | flops 1073741824 | bytes 4194304 | tf_op jit(solution)/shard_map/pallas_call | solution.py:505
  36.4 2.6 %shard_map.142 = (bf16[1024,512]{1,0:T(8,128)(2,1)S(1)}, bf16[512,512]{1,0:T(8,128)(2,1)S(1)}, bf16[512,512]{1,0:T(8,128)(2,1)S(1)}) custom-call(s32[8,8]{1,0:T(8,128)S(1)} %copy-done.9, bf16[1152,512]{1,0:T(8,128)(2,1)S(1)} %get-tuple-element.28.table_ref, bf16[8,8,128,128]{3,2,1,0:T(8,128)(2,1)S(1)} %copy-done, bf16[1024,512]{1,0:T(8,128)(2,1)S(1)} %copy-done.2, ...), custom_call_target="tpu_custom_call" | custom-call | flops 1610612736 | bytes 5242880 | tf_op jit(solution)/shard_map/pallas_call | solution.py:514
  40.1 1.8 %collective-permute-start.24 = (bf16[64,512]{1,0:T(8,128)(2,1)S(1)}, bf16[64,512]{1,0:T(8,128)(2,1)S(1)}, u32[]{:S(2)}, u32[]{:S(2)}) collective-permute-start(bf16[64,512]{1,0:T(8,128)(2,1)S(1)} %pad_maximum_fusion.7), channel_id=1, source_target_pairs={{0,16},{1,17},{2,18},{3,19},{4,20},{5,21},{6,22},{7,23},{8,24},{9,... | collective-permute-start | bytes 196616 | tf_op jit(solution)/shard_map/ppermute | solution.py:59
  42.1 1.6 %collective-permute-start.9 = (bf16[128,512]{1,0:T(8,128)(2,1)S(1)}, bf16[128,512]{1,0:T(8,128)(2,1)S(1)}, u32[]{:S(2)}, u32[]{:S(2)}) collective-permute-start(bf16[128,512]{1,0:T(8,128)(2,1)S(1)} %get-tuple-element.41), channel_id=1, source_target_pairs={{0,4},{1,5},{2,6},{3,7},{4,0},{5,1},{6,2},{7,3},{8,12},{9,13},{10,... | collective-permute-start | bytes 393224 | tf_op jit(solution)/shard_map/ppermute | solution.py:59
  44.2 1.4 %collective-permute-start.11 = (bf16[128,512]{1,0:T(8,128)(2,1)S(1)}, bf16[128,512]{1,0:T(8,128)(2,1)S(1)}, u32[]{:S(2)}, u32[]{:S(2)}) collective-permute-start(bf16[128,512]{1,0:T(8,128)(2,1)S(1)} %get-tuple-element.43), channel_id=1, source_target_pairs={{0,2},{1,3},{2,0},{3,1},{4,6},{5,7},{6,4},{7,5},{8,10},{9,11},{10,... | collective-permute-start | bytes 393224 | tf_op jit(solution)/shard_map/ppermute | solution.py:59
  45.6 2.4 %collective-permute-start.25 = (bf16[64,512]{1,0:T(8,128)(2,1)S(1)}, bf16[64,512]{1,0:T(8,128)(2,1)S(1)}, u32[]{:S(2)}, u32[]{:S(2)}) collective-permute-start(bf16[64,512]{1,0:T(8,128)(2,1)S(1)} %pad_maximum_fusion.8), channel_id=1, source_target_pairs={{0,24},{1,25},{2,26},{3,27},{4,28},{5,29},{6,30},{7,31},{8,16},{9,... | collective-permute-start | bytes 196616 | tf_op jit(solution)/shard_map/ppermute | solution.py:59
  48.5 2.5 %collective-permute-done.13 = bf16[128,512]{1,0:T(8,128)(2,1)S(1)} collective-permute-done((bf16[128,512]{1,0:T(8,128)(2,1)S(1)}, bf16[128,512]{1,0:T(8,128)(2,1)S(1)}, u32[]{:S(2)}, u32[]{:S(2)}) %collective-permute-start.13) | collective-permute-done | bytes 131104 | tf_op jit(solution)/shard_map/ppermute | solution.py:59
  51.0 1.4 %collective-permute-done.11 = bf16[128,512]{1,0:T(8,128)(2,1)S(1)} collective-permute-done((bf16[128,512]{1,0:T(8,128)(2,1)S(1)}, bf16[128,512]{1,0:T(8,128)(2,1)S(1)}, u32[]{:S(2)}, u32[]{:S(2)}) %collective-permute-start.11) | collective-permute-done | bytes 131104 | tf_op jit(solution)/shard_map/ppermute | solution.py:59
  52.5 2.1 %collective-permute-start.16 = (bf16[32,512]{1,0:T(8,128)(2,1)S(1)}, bf16[32,512]{1,0:T(8,128)(2,1)S(1)}, u32[]{:S(2)}, u32[]{:S(2)}) collective-permute-start(bf16[32,512]{1,0:T(8,128)(2,1)S(1)} %get-tuple-element.52), channel_id=1, source_target_pairs={{0,24},{1,25},{2,26},{3,27},{4,28},{5,29},{6,30},{7,31},{8,16},{9,... | collective-permute-start | bytes 98312 | tf_op jit(solution)/shard_map/ppermute | solution.py:59
  54.6 2.3 %collective-permute-start.14 = (bf16[32,512]{1,0:T(8,128)(2,1)S(1)}, bf16[32,512]{1,0:T(8,128)(2,1)S(1)}, u32[]{:S(2)}, u32[]{:S(2)}) collective-permute-start(bf16[32,512]{1,0:T(8,128)(2,1)S(1)} %get-tuple-element.54), channel_id=1, source_target_pairs={{0,8},{1,9},{2,10},{3,11},{4,12},{5,13},{6,14},{7,15},{8,0},{9,1},... | collective-permute-start | bytes 98312 | tf_op jit(solution)/shard_map/ppermute | solution.py:59
  56.9 1.4 %collective-permute-done.16.refs_3_ = bf16[32,512]{1,0:T(8,128)(2,1)S(1)} collective-permute-done((bf16[32,512]{1,0:T(8,128)(2,1)S(1)}, bf16[32,512]{1,0:T(8,128)(2,1)S(1)}, u32[]{:S(2)}, u32[]{:S(2)}) %collective-permute-start.16) | collective-permute-done | bytes 32800 | tf_op jit(solution)/shard_map/ppermute | solution.py:59
  58.3 1.1 %collective-permute-done.15.refs_2_ = bf16[32,512]{1,0:T(8,128)(2,1)S(1)} collective-permute-done((bf16[32,512]{1,0:T(8,128)(2,1)S(1)}, bf16[32,512]{1,0:T(8,128)(2,1)S(1)}, u32[]{:S(2)}, u32[]{:S(2)}) %collective-permute-start.15) | collective-permute-done | bytes 32800 | tf_op jit(solution)/shard_map/ppermute | solution.py:59
  59.5 2.0 %collective-permute-start.19 = (bf16[32,512]{1,0:T(8,128)(2,1)S(1)}, bf16[32,512]{1,0:T(8,128)(2,1)S(1)}, u32[]{:S(2)}, u32[]{:S(2)}) collective-permute-start(bf16[32,512]{1,0:T(8,128)(2,1)S(1)} %shard_map.144), channel_id=1, source_target_pairs={{0,24},{1,25},{2,26},{3,27},{4,28},{5,29},{6,30},{7,31},{8,16},{9,... | collective-permute-start | bytes 98312 | tf_op jit(solution)/shard_map/ppermute | solution.py:59
  62.5 1.5 %collective-permute-start.17 = (bf16[32,512]{1,0:T(8,128)(2,1)S(1)}, bf16[32,512]{1,0:T(8,128)(2,1)S(1)}, u32[]{:S(2)}, u32[]{:S(2)}) collective-permute-start(bf16[32,512]{1,0:T(8,128)(2,1)S(1)} %shard_map.144), channel_id=1, source_target_pairs={{0,8},{1,9},{2,10},{3,11},{4,12},{5,13},{6,14},{7,15},{8,0},{9,1},... | collective-permute-start | bytes 98312 | tf_op jit(solution)/shard_map/ppermute | solution.py:59
  64.0 1.3 %collective-permute-done.19 = bf16[32,512]{1,0:T(8,128)(2,1)S(1)} collective-permute-done((bf16[32,512]{1,0:T(8,128)(2,1)S(1)}, bf16[32,512]{1,0:T(8,128)(2,1)S(1)}, u32[]{:S(2)}, u32[]{:S(2)}) %collective-permute-start.19) | collective-permute-done | bytes 32800 | tf_op jit(solution)/shard_map/ppermute | solution.py:59
  65.3 1.4 %collective-permute-done.18 = bf16[32,512]{1,0:T(8,128)(2,1)S(1)} collective-permute-done((bf16[32,512]{1,0:T(8,128)(2,1)S(1)}, bf16[32,512]{1,0:T(8,128)(2,1)S(1)}, u32[]{:S(2)}, u32[]{:S(2)}) %collective-permute-start.18) | collective-permute-done | bytes 32800 | tf_op jit(solution)/shard_map/ppermute | solution.py:59
  66.7 2.5 %collective-permute-start.22 = (bf16[128,512]{1,0:T(8,128)(2,1)S(1)}, bf16[128,512]{1,0:T(8,128)(2,1)S(1)}, u32[]{:S(2)}, u32[]{:S(2)}) collective-permute-start(bf16[128,512]{1,0:T(8,128)(2,1)S(1)} %pad_maximum_fusion.1), channel_id=1, source_target_pairs={{0,6},{1,7},{2,4},{3,5},{4,2},{5,3},{6,0},{7,1},{8,14},{9,15},{10,... | collective-permute-start | bytes 393224 | tf_op jit(solution)/shard_map/ppermute | solution.py:59
  70.2 4.4 %collective-permute-done.20 = bf16[128,512]{1,0:T(8,128)(2,1)S(1)} collective-permute-done((bf16[128,512]{1,0:T(8,128)(2,1)S(1)}, bf16[128,512]{1,0:T(8,128)(2,1)S(1)}, u32[]{:S(2)}, u32[]{:S(2)}) %collective-permute-start.20) | collective-permute-done | bytes 131104 | tf_op jit(solution)/shard_map/ppermute | solution.py:59
  75.9 1.7 %shard_map.143 = bf16[1024,512]{1,0:T(8,128)(2,1)} custom-call(bf16[1024,512]{1,0:T(8,128)(2,1)S(1)} %get-tuple-element.30.p_ref, bf16[512,512]{1,0:T(8,128)(2,1)S(1)} %constant_dynamic-update-slice_fusion.13.lo_ref, bf16[512,512]{1,0:T(8,128)(2,1)S(1)} %collective-permute-done.6.hi_ref), custom_call_target="tpu_custom_call" | custom-call | flops 536870912 | bytes 2097152 | tf_op jit(solution)/shard_map/pallas_call | solution.py:524
  77.7 3.2 %collective-permute-done.26 = bf16[128,512]{1,0:T(8,128)(2,1)S(1)} collective-permute-done((bf16[128,512]{1,0:T(8,128)(2,1)S(1)}, bf16[128,512]{1,0:T(8,128)(2,1)S(1)}, u32[]{:S(2)}, u32[]{:S(2)}) %collective-permute-start.26) | collective-permute-done | bytes 131104 | tf_op jit(solution)/shard_map/ppermute | solution.py:59
  81.6 1.3 %shard_map.145 = (bf16[2,512,512]{2,1,0:T(8,128)(2,1)}, bf16[128,512]{1,0:T(8,128)(2,1)}, bf16[128,512]{1,0:T(8,128)(2,1)}) custom-call(bf16[512,512]{1,0:T(8,128)(2,1)S(1)} %constant_dynamic-update-slice_fusion.19.part_ref, bf16[256,512]{1,0:T(8,128)(2,1)S(1)} %constant_dynamic-update-slice_fusion.26.fresh_ref), custom_call_target="tpu_custom_call" | custom-call | bytes 1048576 | tf_op jit(solution)/shard_map/pallas_call | solution.py:551
  (91 shorter events, 9.1 us)
Async XLA Ops:
  0.6 23.6 %copy-start.9 = (s32[8,8]{1,0:T(8,128)S(1)}, s32[8,8]{1,0:T(8,128)}, u32[]{:S(2)}) copy-start(s32[8,8]{1,0:T(8,128)} %src_ref.5) | copy-start | bytes 772
  2.4 25.4 %copy-start = (bf16[8,8,128,128]{3,2,1,0:T(8,128)(2,1)S(1)}, bf16[8,8,128,128]{3,2,1,0:T(8,128)(2,1)}, u32[]{:S(2)}) copy-start(bf16[8,8,128,128]{3,2,1,0:T(8,128)(2,1)} %tile_ref.3) | copy-start | bytes 6291460
  2.4 25.4 %copy-start.1 = (bf16[1024,512]{1,0:T(8,128)(2,1)S(1)}, bf16[1024,512]{1,0:T(8,128)(2,1)}, u32[]{:S(2)}) copy-start(bf16[1024,512]{1,0:T(8,128)(2,1)} %feat_ref.1) | copy-start | bytes 3145732
  2.5 10.8 %collective-permute-start.2 = (bf16[64,512]{1,0:T(8,128)(2,1)S(1)}, bf16[64,512]{1,0:T(8,128)(2,1)S(1)}, u32[]{:S(2)}, u32[]{:S(2)}) collective-permute-start(bf16[64,512]{1,0:T(8,128)(2,1)S(1)} %get-tuple-element.87), channel_id=1, source_target_pairs={{0,24},{1,25},{2,26},{3,27},{4,28},{5,29},{6,30},{7,31},{8,16},{9,... | collective-permute-start | bytes 196616 | tf_op jit(solution)/shard_map/ppermute | solution.py:59
  7.6 5.6 %collective-permute-start.1 = (bf16[64,512]{1,0:T(8,128)(2,1)S(1)}, bf16[64,512]{1,0:T(8,128)(2,1)S(1)}, u32[]{:S(2)}, u32[]{:S(2)}) collective-permute-start(bf16[64,512]{1,0:T(8,128)(2,1)S(1)} %get-tuple-element.88), channel_id=1, source_target_pairs={{0,16},{1,17},{2,18},{3,19},{4,20},{5,21},{6,22},{7,23},{8,24},{9,... | collective-permute-start | bytes 196616 | tf_op jit(solution)/shard_map/ppermute | solution.py:59
  7.6 4.3 %collective-permute-start = (bf16[64,512]{1,0:T(8,128)(2,1)S(1)}, bf16[64,512]{1,0:T(8,128)(2,1)S(1)}, u32[]{:S(2)}, u32[]{:S(2)}) collective-permute-start(bf16[64,512]{1,0:T(8,128)(2,1)S(1)} %get-tuple-element.89), channel_id=1, source_target_pairs={{0,8},{1,9},{2,10},{3,11},{4,12},{5,13},{6,14},{7,15},{8,0},{9,1},... | collective-permute-start | bytes 196616 | tf_op jit(solution)/shard_map/ppermute | solution.py:59
  13.3 7.8 %collective-permute-start.3 = (bf16[192,512]{1,0:T(8,128)(2,1)S(1)}, bf16[192,512]{1,0:T(8,128)(2,1)S(1)}, u32[]{:S(2)}, u32[]{:S(2)}) collective-permute-start(bf16[192,512]{1,0:T(8,128)(2,1)S(1)} %get-tuple-element.79), channel_id=1, source_target_pairs={{0,4},{1,5},{2,6},{3,7},{4,0},{5,1},{6,2},{7,3},{8,12},{9,13},{10,... | collective-permute-start | bytes 589832 | tf_op jit(solution)/shard_map/ppermute | solution.py:59
  14.9 9.2 %collective-permute-start.5 = (bf16[128,512]{1,0:T(8,128)(2,1)S(1)}, bf16[128,512]{1,0:T(8,128)(2,1)S(1)}, u32[]{:S(2)}, u32[]{:S(2)}) collective-permute-start(bf16[128,512]{1,0:T(8,128)(2,1)S(1)} %pad_maximum_fusion), channel_id=1, source_target_pairs={{0,6},{1,7},{2,4},{3,5},{4,2},{5,3},{6,0},{7,1},{8,14},{9,15},{10,... | collective-permute-start | bytes 393224 | tf_op jit(solution)/shard_map/ppermute | solution.py:59
  16.4 7.6 %collective-permute-start.4 = (bf16[128,512]{1,0:T(8,128)(2,1)S(1)}, bf16[128,512]{1,0:T(8,128)(2,1)S(1)}, u32[]{:S(2)}, u32[]{:S(2)}) collective-permute-start(bf16[128,512]{1,0:T(8,128)(2,1)S(1)} %pad_maximum_fusion), channel_id=1, source_target_pairs={{0,2},{1,3},{2,0},{3,1},{4,6},{5,7},{6,4},{7,5},{8,10},{9,11},{10,... | collective-permute-start | bytes 393224 | tf_op jit(solution)/shard_map/ppermute | solution.py:59
  24.1 5.9 %collective-permute-start.6 = (bf16[512,512]{1,0:T(8,128)(2,1)S(1)}, bf16[512,512]{1,0:T(8,128)(2,1)S(1)}, u32[]{:S(2)}, u32[]{:S(2)}) collective-permute-start(bf16[512,512]{1,0:T(8,128)(2,1)S(1)} %constant_dynamic-update-slice_fusion.13.lo_ref), channel_id=1, source_target_pairs={{0,1},{1,0},{2,3},{3,2},{4,5},{5,4},{6,7},{7,6},{8,9},{9,8},{10,11... | collective-permute-start | bytes 1572872 | tf_op jit(solution)/shard_map/ppermute | solution.py:59
  36.2 8.0 %collective-permute-start.23 = (bf16[64,512]{1,0:T(8,128)(2,1)S(1)}, bf16[64,512]{1,0:T(8,128)(2,1)S(1)}, u32[]{:S(2)}, u32[]{:S(2)}) collective-permute-start(bf16[64,512]{1,0:T(8,128)(2,1)S(1)} %pad_maximum_fusion.6), channel_id=1, source_target_pairs={{0,8},{1,9},{2,10},{3,11},{4,12},{5,13},{6,14},{7,15},{8,0},{9,1},... | collective-permute-start | bytes 196616 | tf_op jit(solution)/shard_map/ppermute | solution.py:59
  39.0 20.5 %copy-start.3 = (f32[2,16,512]{2,1,0:T(8,128)S(1)}, f32[2,16,512]{2,1,0:T(8,128)}, u32[]{:S(2)}) copy-start(f32[2,16,512]{2,1,0:T(8,128)} %refs_4_.3) | copy-start | bytes 196612
  39.0 2.8 %collective-permute-start.12 = (bf16[128,512]{1,0:T(8,128)(2,1)S(1)}, bf16[128,512]{1,0:T(8,128)(2,1)S(1)}, u32[]{:S(2)}, u32[]{:S(2)}) collective-permute-start(bf16[128,512]{1,0:T(8,128)(2,1)S(1)} %get-tuple-element.38), channel_id=1, source_target_pairs={{0,1},{1,0},{2,3},{3,2},{4,5},{5,4},{6,7},{7,6},{8,9},{9,8},{10,11... | collective-permute-start | bytes 393224 | tf_op jit(solution)/shard_map/ppermute | solution.py:59
  39.5 2.4 %collective-permute-start.10 = (bf16[128,512]{1,0:T(8,128)(2,1)S(1)}, bf16[128,512]{1,0:T(8,128)(2,1)S(1)}, u32[]{:S(2)}, u32[]{:S(2)}) collective-permute-start(bf16[128,512]{1,0:T(8,128)(2,1)S(1)} %get-tuple-element.39), channel_id=1, source_target_pairs={{0,1},{1,0},{2,3},{3,2},{4,5},{5,4},{6,7},{7,6},{8,9},{9,8},{10,11... | collective-permute-start | bytes 393224 | tf_op jit(solution)/shard_map/ppermute | solution.py:59
  39.6 2.3 %collective-permute-start.8 = (bf16[128,512]{1,0:T(8,128)(2,1)S(1)}, bf16[128,512]{1,0:T(8,128)(2,1)S(1)}, u32[]{:S(2)}, u32[]{:S(2)}) collective-permute-start(bf16[128,512]{1,0:T(8,128)(2,1)S(1)} %get-tuple-element.40), channel_id=1, source_target_pairs={{0,1},{1,0},{2,3},{3,2},{4,5},{5,4},{6,7},{7,6},{8,9},{9,8},{10,11... | collective-permute-start | bytes 393224 | tf_op jit(solution)/shard_map/ppermute | solution.py:59
  40.1 16.9 %collective-permute-start.24 = (bf16[64,512]{1,0:T(8,128)(2,1)S(1)}, bf16[64,512]{1,0:T(8,128)(2,1)S(1)}, u32[]{:S(2)}, u32[]{:S(2)}) collective-permute-start(bf16[64,512]{1,0:T(8,128)(2,1)S(1)} %pad_maximum_fusion.7), channel_id=1, source_target_pairs={{0,16},{1,17},{2,18},{3,19},{4,20},{5,21},{6,22},{7,23},{8,24},{9,... | collective-permute-start | bytes 196616 | tf_op jit(solution)/shard_map/ppermute | solution.py:59
  41.8 3.8 %collective-permute-start.7 = (bf16[128,512]{1,0:T(8,128)(2,1)S(1)}, bf16[128,512]{1,0:T(8,128)(2,1)S(1)}, u32[]{:S(2)}, u32[]{:S(2)}) collective-permute-start(bf16[128,512]{1,0:T(8,128)(2,1)S(1)} %get-tuple-element.37), channel_id=1, source_target_pairs={{0,1},{1,0},{2,3},{3,2},{4,5},{5,4},{6,7},{7,6},{8,9},{9,8},{10,11... | collective-permute-start | bytes 393224 | tf_op jit(solution)/shard_map/ppermute | solution.py:59
  42.1 6.4 %collective-permute-start.9 = (bf16[128,512]{1,0:T(8,128)(2,1)S(1)}, bf16[128,512]{1,0:T(8,128)(2,1)S(1)}, u32[]{:S(2)}, u32[]{:S(2)}) collective-permute-start(bf16[128,512]{1,0:T(8,128)(2,1)S(1)} %get-tuple-element.41), channel_id=1, source_target_pairs={{0,4},{1,5},{2,6},{3,7},{4,0},{5,1},{6,2},{7,3},{8,12},{9,13},{10,... | collective-permute-start | bytes 393224 | tf_op jit(solution)/shard_map/ppermute | solution.py:59
  43.6 7.4 %collective-permute-start.13 = (bf16[128,512]{1,0:T(8,128)(2,1)S(1)}, bf16[128,512]{1,0:T(8,128)(2,1)S(1)}, u32[]{:S(2)}, u32[]{:S(2)}) collective-permute-start(bf16[128,512]{1,0:T(8,128)(2,1)S(1)} %get-tuple-element.42), channel_id=1, source_target_pairs={{0,6},{1,7},{2,4},{3,5},{4,2},{5,3},{6,0},{7,1},{8,14},{9,15},{10,... | collective-permute-start | bytes 393224 | tf_op jit(solution)/shard_map/ppermute | solution.py:59
  44.2 8.1 %collective-permute-start.11 = (bf16[128,512]{1,0:T(8,128)(2,1)S(1)}, bf16[128,512]{1,0:T(8,128)(2,1)S(1)}, u32[]{:S(2)}, u32[]{:S(2)}) collective-permute-start(bf16[128,512]{1,0:T(8,128)(2,1)S(1)} %get-tuple-element.43), channel_id=1, source_target_pairs={{0,2},{1,3},{2,0},{3,1},{4,6},{5,7},{6,4},{7,5},{8,10},{9,11},{10,... | collective-permute-start | bytes 393224 | tf_op jit(solution)/shard_map/ppermute | solution.py:59
  45.6 29.2 %collective-permute-start.25 = (bf16[64,512]{1,0:T(8,128)(2,1)S(1)}, bf16[64,512]{1,0:T(8,128)(2,1)S(1)}, u32[]{:S(2)}, u32[]{:S(2)}) collective-permute-start(bf16[64,512]{1,0:T(8,128)(2,1)S(1)} %pad_maximum_fusion.8), channel_id=1, source_target_pairs={{0,24},{1,25},{2,26},{3,27},{4,28},{5,29},{6,30},{7,31},{8,16},{9,... | collective-permute-start | bytes 196616 | tf_op jit(solution)/shard_map/ppermute | solution.py:59
  52.5 5.9 %collective-permute-start.16 = (bf16[32,512]{1,0:T(8,128)(2,1)S(1)}, bf16[32,512]{1,0:T(8,128)(2,1)S(1)}, u32[]{:S(2)}, u32[]{:S(2)}) collective-permute-start(bf16[32,512]{1,0:T(8,128)(2,1)S(1)} %get-tuple-element.52), channel_id=1, source_target_pairs={{0,24},{1,25},{2,26},{3,27},{4,28},{5,29},{6,30},{7,31},{8,16},{9,... | collective-permute-start | bytes 98312 | tf_op jit(solution)/shard_map/ppermute | solution.py:59
  54.6 4.8 %collective-permute-start.15 = (bf16[32,512]{1,0:T(8,128)(2,1)S(1)}, bf16[32,512]{1,0:T(8,128)(2,1)S(1)}, u32[]{:S(2)}, u32[]{:S(2)}) collective-permute-start(bf16[32,512]{1,0:T(8,128)(2,1)S(1)} %get-tuple-element.53), channel_id=1, source_target_pairs={{0,16},{1,17},{2,18},{3,19},{4,20},{5,21},{6,22},{7,23},{8,24},{9,... | collective-permute-start | bytes 98312 | tf_op jit(solution)/shard_map/ppermute | solution.py:59
  54.6 4.8 %collective-permute-start.14 = (bf16[32,512]{1,0:T(8,128)(2,1)S(1)}, bf16[32,512]{1,0:T(8,128)(2,1)S(1)}, u32[]{:S(2)}, u32[]{:S(2)}) collective-permute-start(bf16[32,512]{1,0:T(8,128)(2,1)S(1)} %get-tuple-element.54), channel_id=1, source_target_pairs={{0,8},{1,9},{2,10},{3,11},{4,12},{5,13},{6,14},{7,15},{8,0},{9,1},... | collective-permute-start | bytes 98312 | tf_op jit(solution)/shard_map/ppermute | solution.py:59
  59.5 5.8 %collective-permute-start.19 = (bf16[32,512]{1,0:T(8,128)(2,1)S(1)}, bf16[32,512]{1,0:T(8,128)(2,1)S(1)}, u32[]{:S(2)}, u32[]{:S(2)}) collective-permute-start(bf16[32,512]{1,0:T(8,128)(2,1)S(1)} %shard_map.144), channel_id=1, source_target_pairs={{0,24},{1,25},{2,26},{3,27},{4,28},{5,29},{6,30},{7,31},{8,16},{9,... | collective-permute-start | bytes 98312 | tf_op jit(solution)/shard_map/ppermute | solution.py:59
  61.5 5.2 %collective-permute-start.18 = (bf16[32,512]{1,0:T(8,128)(2,1)S(1)}, bf16[32,512]{1,0:T(8,128)(2,1)S(1)}, u32[]{:S(2)}, u32[]{:S(2)}) collective-permute-start(bf16[32,512]{1,0:T(8,128)(2,1)S(1)} %shard_map.144), channel_id=1, source_target_pairs={{0,16},{1,17},{2,18},{3,19},{4,20},{5,21},{6,22},{7,23},{8,24},{9,... | collective-permute-start | bytes 98312 | tf_op jit(solution)/shard_map/ppermute | solution.py:59
  62.5 4.2 %collective-permute-start.17 = (bf16[32,512]{1,0:T(8,128)(2,1)S(1)}, bf16[32,512]{1,0:T(8,128)(2,1)S(1)}, u32[]{:S(2)}, u32[]{:S(2)}) collective-permute-start(bf16[32,512]{1,0:T(8,128)(2,1)S(1)} %shard_map.144), channel_id=1, source_target_pairs={{0,8},{1,9},{2,10},{3,11},{4,12},{5,13},{6,14},{7,15},{8,0},{9,1},... | collective-permute-start | bytes 98312 | tf_op jit(solution)/shard_map/ppermute | solution.py:59
  66.7 8.1 %collective-permute-start.22 = (bf16[128,512]{1,0:T(8,128)(2,1)S(1)}, bf16[128,512]{1,0:T(8,128)(2,1)S(1)}, u32[]{:S(2)}, u32[]{:S(2)}) collective-permute-start(bf16[128,512]{1,0:T(8,128)(2,1)S(1)} %pad_maximum_fusion.1), channel_id=1, source_target_pairs={{0,6},{1,7},{2,4},{3,5},{4,2},{5,3},{6,0},{7,1},{8,14},{9,15},{10,... | collective-permute-start | bytes 393224 | tf_op jit(solution)/shard_map/ppermute | solution.py:59
  69.2 5.5 %collective-permute-start.21 = (bf16[128,512]{1,0:T(8,128)(2,1)S(1)}, bf16[128,512]{1,0:T(8,128)(2,1)S(1)}, u32[]{:S(2)}, u32[]{:S(2)}) collective-permute-start(bf16[128,512]{1,0:T(8,128)(2,1)S(1)} %pad_maximum_fusion.1), channel_id=1, source_target_pairs={{0,2},{1,3},{2,0},{3,1},{4,6},{5,7},{6,4},{7,5},{8,10},{9,11},{10,... | collective-permute-start | bytes 393224 | tf_op jit(solution)/shard_map/ppermute | solution.py:59
  69.7 5.0 %collective-permute-start.20 = (bf16[128,512]{1,0:T(8,128)(2,1)S(1)}, bf16[128,512]{1,0:T(8,128)(2,1)S(1)}, u32[]{:S(2)}, u32[]{:S(2)}) collective-permute-start(bf16[128,512]{1,0:T(8,128)(2,1)S(1)} %pad_maximum_fusion.1), channel_id=1, source_target_pairs={{0,4},{1,5},{2,6},{3,7},{4,0},{5,1},{6,2},{7,3},{8,12},{9,13},{10,... | collective-permute-start | bytes 393224 | tf_op jit(solution)/shard_map/ppermute | solution.py:59
  74.8 8.1 %collective-permute-start.27 = (bf16[512,512]{1,0:T(8,128)(2,1)S(1)}, bf16[512,512]{1,0:T(8,128)(2,1)S(1)}, u32[]{:S(2)}, u32[]{:S(2)}) collective-permute-start(bf16[512,512]{1,0:T(8,128)(2,1)S(1)} %constant_dynamic-update-slice_fusion.19.part_ref), channel_id=1, source_target_pairs={{0,1},{1,0},{2,3},{3,2},{4,5},{5,4},{6,7},{7,6},{8,9},{9,8},{10,11... | collective-permute-start | bytes 1572872 | tf_op jit(solution)/shard_map/ppermute | solution.py:59
  74.9 6.0 %collective-permute-start.26 = (bf16[128,512]{1,0:T(8,128)(2,1)S(1)}, bf16[128,512]{1,0:T(8,128)(2,1)S(1)}, u32[]{:S(2)}, u32[]{:S(2)}) collective-permute-start(bf16[128,512]{1,0:T(8,128)(2,1)S(1)} %pad_maximum_fusion.2), channel_id=1, source_target_pairs={{0,4},{1,5},{2,6},{3,7},{4,0},{5,1},{6,2},{7,3},{8,12},{9,13},{10,... | collective-permute-start | bytes 393224 | tf_op jit(solution)/shard_map/ppermute | solution.py:59
  (6 other events, 51.1 us)

commit v2 on v1

--- a/solution.py
+++ b/solution.py
@@ -46,16 +46,27 @@
     return stages
 
 
+def cross_stages(stages):
+    if len(stages) < 3 or len(stages[1]) != len(stages[2]):
+        return stages
+    pairs = (stages[1], stages[2]), (stages[2], stages[1])
+    return [stages[0]] + [[m + n for m, n in zip(*p)] for p in pairs] + stages[3:]
+
+
 def relative_order(stages):
-    order = [(0, 0)]
+    order = [(0, 0, 0, 0)]
     for members in stages:
-        order = [(a ^ x, b ^ y) for a, b in order for x, y in members]
+        wide = [m if len(m) == 4 else m + m for m in members]
+        order = [tuple(x ^ y for x, y in zip(at, m[2:] + m[:2] if at[1] % 2 else m)) for at in order for m in wide]
     return order
 
 
 def swap(x, mask):
     nd, ng = lax.axis_size("dom"), lax.axis_size("grp")
-    pairs = [(k, ((k // ng) ^ mask[0]) * ng + ((k % ng) ^ mask[1])) for k in range(nd * ng)]
+    pairs = []
+    for k in range(nd * ng):
+        a, b = mask[-2:] if k % 2 else mask[:2]
+        pairs.append((k, ((k // ng) ^ a) * ng + ((k % ng) ^ b)))
     return lax.ppermute(x, AXES, pairs)
 
 
@@ -105,18 +116,24 @@
 
 
 class Layout:
-    def __init__(self, nd, ng, shard_rows):
+    def __init__(self, nd, ng, shard_rows, crossed=False):
         self.stages = plan_stages(nd, ng)
         self.ways = dom_stages(self.stages)
+        if crossed:
+            self.stages = cross_stages(self.stages)
         self.blocks = relative_order(self.stages)
-        self.peers = [a for a, _ in relative_order(self.ways)]
+        self.peers = [m[0] for m in relative_order(self.ways)]
         self.ng = ng
         self.packed = shard_rows % PACK == 0
         self.count = nd * ng if self.packed else nd * ng * shard_rows // PACK
 
     def owner(self, r):
-        a, b = self.blocks[r]
-        return (lax.axis_index("dom") ^ a) * self.ng + (lax.axis_index("grp") ^ b)
+        a, b, c, d = self.blocks[r]
+        group = lax.axis_index("grp")
+        if (a, b) != (c, d):
+            odd = group % 2
+            a, b = a + odd * (c - a), b + odd * (d - b)
+        return (lax.axis_index("dom") ^ a) * self.ng + (group ^ b)
 
     def block(self, r):
         return self.owner(r) if self.packed else r
@@ -415,11 +432,12 @@
     slots = blocks + rim // edge
     selects = send_sel[0]
     lay = Layout(peers, groups, shard_rows)
+    turned = Layout(peers, groups, shard_rows, True)
     count, size = lay.count, full_rows // lay.count
     half = layers * full_rows // 2
     sds = jax.ShapeDtypeStruct
 
-    def spread_out(lo, hi):
+    def spread_out(lay, lo, hi):
         if lay.packed:
             return lo, hi
         owner = jnp.stack([lay.owner(r) for r in range(devices)])
@@ -429,7 +447,7 @@
         whole = whole.transpose(1, 0, 2, 3).reshape(layers * full_rows, width)
         return whole[:half], whole[half:]
 
-    def draw_in(keep, send):
+    def draw_in(lay, keep, send):
         if lay.packed:
             return keep, send
         owner = jnp.stack([lay.owner(r) for r in range(devices)])
@@ -464,7 +482,7 @@
     lo, hi, raw_rim = gather_relative(
         own.reshape(layers * shard_rows, width), lay.stages, jnp.split(picked, peers, 0), lay.ways
     )
-    lo, hi = spread_out(lo, hi)
+    lo, hi = spread_out(lay, lo, hi)
     raw_rim = jnp.concatenate(raw_rim, 0)
     turned_tiles, order, goal, _ = call(
         prepare_kernel,
@@ -512,7 +530,7 @@
         4 * node_bytes,
     )(selects, p_first, p_turned, acc, stale_features, lo, hi)
     p_second, keep, send = call(
-        part(second_kernel, lay),
+        part(second_kernel, turned),
         (nodes, grads_half, grads_half),
         [SMEM, VMEM, VMEM, VMEM, VMEM],
         (VMEM, VMEM, VMEM),
@@ -520,7 +538,7 @@
         tile_flops + dense_flops,
         tile_bytes + 3 * node_bytes,
     )(tile_src, sources, tile_val, out_grad, g_first)
-    total = reduce_relative(*draw_in(keep, send), lay.stages)
+    total = reduce_relative(*draw_in(turned, keep, send), turned.stages)
     layer_out = call(
         part(out_kernel, lay),
         nodes,
@@ -545,11 +563,11 @@
     master_next = call(
         part(settle_kernel, total_nodes), sds(master.shape, F32), [VMEM] * len(state), VMEM, [], 0, 12 * master.size
     )(*state)
-    lo_next, hi_next, _ = gather_relative(moved, lay.stages)
-    lo_next, hi_next = spread_out(lo_next, hi_next)
+    lo_next, hi_next, _ = gather_relative(moved, turned.stages)
+    lo_next, hi_next = spread_out(turned, lo_next, hi_next)
     weights = sds((layers, full_rows, width), BF16)
     weights_next, fresh_features, fresh_grads = call(
-        part(place_kernel, lay),
+        part(place_kernel, turned),
         (weights, sds((rim, width), BF16), sds((rim, width), BF16)),
         [VMEM, VMEM],
         (HBM, HBM, HBM),
@@ -558,7 +576,7 @@
         2 * layers * full_rows * width,
     )(lo_next, fresh)
     weights_next = call(
-        part(finish_kernel, lay),
+        part(finish_kernel, turned),
         weights,
         [VMEM, HBM],
         HBM,

time: 84.2 us -> 81.9 us (0.973)
  waiting for transfers between devices: 29.2 us -> 25.8 us
  starting transfers between devices: 32 us -> 33.1 us
    ppermute x28, waiting for transfers between devices: 29.2 us -> 25.8 us  [swap(): return lax.ppermute(x, AXES, pairs)]
    ppermute x28, starting transfers between devices: 32 us -> 33.1 us  [swap(): return lax.ppermute(x, AXES, pairs)]
  transfers between devices with their start and end apart: 28 -> 28, of which waited for: 13 -> 12; matrix products, arithmetic and copies ran while one was open for 0% -> 0% of each run, Pallas kernels for 14% -> 15%
where the time goes in v2:
time: 81.9 us; the launch traced here: 81.6 us
  starting transfers between devices  33.1 us (40%)
  waiting for transfers between devices  25.8 us (32%)
  Pallas kernels  21.1 us (26%)
  between operations  1.11 us (1%)
    ppermute x28, starting transfers between devices, swap(): return lax.ppermute(x, AXES, pairs)  33.1 us
    ppermute x28, waiting for transfers between devices, swap(): return lax.ppermute(x, AXES, pairs)  25.8 us
    pallas_call x1, Pallas kernels, epoch(): call(prepare_kernel, (sds((blocks * tiles + 1, edge, edge), BF16), sds((l...  3.56 us
    pallas_call x1, Pallas kernels, epoch(): call(part(spread_kernel, lay), sds((local + rim, width), F32), [SMEM, SME...  3.54 us
    pallas_call x1, Pallas kernels, epoch(): call(part(second_kernel, turned), (nodes, grads_half, grads_half), [SMEM,...  2.61 us
    pallas_call x1, Pallas kernels, epoch(): call(part(hidden_kernel, lay), (sds((local + rim, width), BF16), sds((2 *...  2.6 us
    pallas_call x1, Pallas kernels, epoch(): call(part(first_kernel, lay), (nodes, sds((width, local), BF16)), [SMEM,...  2.13 us
    pallas_call x1, Pallas kernels, epoch(): call(part(out_kernel, lay), nodes, [VMEM, VMEM, VMEM], VMEM, [pltpu.VMEM(...  1.75 us
  transfers between devices with their start and end apart: 28, of which 12 were waited for; matrix products, arithmetic and copies ran while one was open for 0% of the time, Pallas kernels for 15%

profile of v2, /device:TPU:0, one launch (start us, length us, event | category | flops | bytes accessed | tf_op | source)
XLA Modules:
  0.0 81.6 jit_solution(14282775315151831597)
XLA Ops:
  0.6 1.7 %shard_map.137 = (bf16[2,16,512]{2,1,0:T(8,128)(2,1)S(1)}, bf16[128,512]{1,0:T(8,128)(2,1)S(1)}) custom-call(s32[1,8]{1,0:T(1,128)} %sel_hbm.1, f32[2,16,512]{2,1,0:T(8,128)} %refs_4_.3, bf16[1024,512]{1,0:T(8,128)(2,1)} %feat_ref.1), custom_call_target="tpu_custom_call" | custom-call | bytes 262144 | tf_op jit(solution)/shard_map/pallas_call | solution.py:469
  2.5 5.1 %collective-permute-start.2 = (bf16[64,512]{1,0:T(8,128)(2,1)S(1)}, bf16[64,512]{1,0:T(8,128)(2,1)S(1)}, u32[]{:S(2)}, u32[]{:S(2)}) collective-permute-start(bf16[64,512]{1,0:T(8,128)(2,1)S(1)} %get-tuple-element.87), channel_id=1, source_target_pairs={{0,24},{1,25},{2,26},{3,27},{4,28},{5,29},{6,30},{7,31},{8,16},{9,... | collective-permute-start | bytes 196616 | tf_op jit(solution)/shard_map/ppermute | solution.py:70
  8.2 3.6 %collective-permute-done = bf16[64,512]{1,0:T(8,128)(2,1)S(1)} collective-permute-done((bf16[64,512]{1,0:T(8,128)(2,1)S(1)}, bf16[64,512]{1,0:T(8,128)(2,1)S(1)}, u32[]{:S(2)}, u32[]{:S(2)}) %collective-permute-start) | collective-permute-done | bytes 65568 | tf_op jit(solution)/shard_map/ppermute | solution.py:70
  11.9 1.3 %collective-permute-done.1 = bf16[64,512]{1,0:T(8,128)(2,1)S(1)} collective-permute-done((bf16[64,512]{1,0:T(8,128)(2,1)S(1)}, bf16[64,512]{1,0:T(8,128)(2,1)S(1)}, u32[]{:S(2)}, u32[]{:S(2)}) %collective-permute-start.1) | collective-permute-done | bytes 65568 | tf_op jit(solution)/shard_map/ppermute | solution.py:70
  13.3 1.6 %collective-permute-start.3 = (bf16[192,512]{1,0:T(8,128)(2,1)S(1)}, bf16[192,512]{1,0:T(8,128)(2,1)S(1)}, u32[]{:S(2)}, u32[]{:S(2)}) collective-permute-start(bf16[192,512]{1,0:T(8,128)(2,1)S(1)} %get-tuple-element.79), channel_id=1, source_target_pairs={{0,4},{1,5},{2,6},{3,7},{4,0},{5,1},{6,2},{7,3},{8,12},{9,13},{10,... | collective-permute-start | bytes 589832 | tf_op jit(solution)/shard_map/ppermute | solution.py:70
  14.9 1.6 %collective-permute-start.5 = (bf16[128,512]{1,0:T(8,128)(2,1)S(1)}, bf16[128,512]{1,0:T(8,128)(2,1)S(1)}, u32[]{:S(2)}, u32[]{:S(2)}) collective-permute-start(bf16[128,512]{1,0:T(8,128)(2,1)S(1)} %pad_maximum_fusion), channel_id=1, source_target_pairs={{0,6},{1,7},{2,4},{3,5},{4,2},{5,3},{6,0},{7,1},{8,14},{9,15},{10,... | collective-permute-start | bytes 393224 | tf_op jit(solution)/shard_map/ppermute | solution.py:70
  16.9 4.2 %collective-permute-done.3 = bf16[192,512]{1,0:T(8,128)(2,1)S(1)} collective-permute-done((bf16[192,512]{1,0:T(8,128)(2,1)S(1)}, bf16[192,512]{1,0:T(8,128)(2,1)S(1)}, u32[]{:S(2)}, u32[]{:S(2)}) %collective-permute-start.3) | collective-permute-done | bytes 196640 | tf_op jit(solution)/shard_map/ppermute | solution.py:70
  21.1 2.9 %collective-permute-done.4 = bf16[128,512]{1,0:T(8,128)(2,1)S(1)} collective-permute-done((bf16[128,512]{1,0:T(8,128)(2,1)S(1)}, bf16[128,512]{1,0:T(8,128)(2,1)S(1)}, u32[]{:S(2)}, u32[]{:S(2)}) %collective-permute-start.4) | collective-permute-done | bytes 131104 | tf_op jit(solution)/shard_map/ppermute | solution.py:70
  24.2 3.6 %shard_map.139 = (bf16[65,128,128]{2,1,0:T(8,128)(2,1)S(1)}, s32[88]{0:T(128)S(1)}, s32[22]{0:T(128)S(1)}, s32[2]{0:T(128)}) custom-call(s32[8,8]{1,0:T(8,128)S(1)} %copy-done.9, bf16[8,8,128,128]{3,2,1,0:T(8,128)(2,1)} %tile_ref.3), custom_call_target="tpu_custom_call" | custom-call | bytes 4194304 | tf_op jit(solution)/shard_map/pallas_call | solution.py:487
  27.8 2.1 %shard_map.138 = (bf16[1024,512]{1,0:T(8,128)(2,1)S(1)}, bf16[512,1024]{1,0:T(8,128)(2,1)S(1)}) custom-call(s32[8,8]{1,0:T(8,128)S(1)} %copy-done.9, bf16[1024,512]{1,0:T(8,128)(2,1)S(1)} %copy-done.1, bf16[128,512]{1,0:T(8,128)(2,1)S(1)} %constant_dynamic-update-slice_fusion.8.rim_ref, bf16[8,8,128,128]{3,2,1,0:T(8,128)(2,1)S(1)} %copy-done), custom_call_target="tpu_custom_call" | custom-call | flops 1073741824 | bytes 4194304 | tf_op jit(solution)/shard_map/pallas_call | solution.py:505
  30.0 3.5 %shard_map.140.acc_ref = f32[1152,512]{1,0:T(8,128)S(1)} custom-call(s32[88]{0:T(128)S(1)} %get-tuple-element.25.list_ref, s32[22]{0:T(128)S(1)} %get-tuple-element.26.goal_ref, s32[8]{0:T(128)S(1)} %bitcast.5, bf16[1024,512]{1,0:T(8,128)(2,1)S(1)} %copy-done.2, bf16[65,128,128]{2,1,0:T(8,128)(2,1)S(1)} %get-tuple-element.27.turned_ref, ...), custom_call_target="tpu_custom_call" | custom-call | flops 1610612736 | bytes 5242880 | tf_op jit(solution)/shard_map/pallas_call | solution.py:514
  33.6 2.6 %shard_map.141 = (bf16[1152,512]{1,0:T(8,128)(2,1)S(1)}, bf16[256,512]{1,0:T(8,128)(2,1)S(1)}, f32[512,512]{1,0:T(8,128)S(1)}) custom-call(s32[8]{0:T(128)S(1)} %bitcast.6, bf16[1024,512]{1,0:T(8,128)(2,1)S(1)} %get-tuple-element.23.p_ref, bf16[512,1024]{1,0:T(8,128)(2,1)S(1)} %get-tuple-element.24.turned_ref, f32[1152,512]{1,0:T(8,128)S(1)} %shard_map.140.acc_ref, ...), custom_call_target="tpu_custom_call" | custom-call | flops 1073741824 | bytes 4194304 | tf_op jit(solution)/shard_map/pallas_call | solution.py:523
  36.4 2.6 %shard_map.142 = (bf16[1024,512]{1,0:T(8,128)(2,1)S(1)}, bf16[512,512]{1,0:T(8,128)(2,1)S(1)}, bf16[512,512]{1,0:T(8,128)(2,1)S(1)}) custom-call(s32[8,8]{1,0:T(8,128)S(1)} %copy-done.9, bf16[1152,512]{1,0:T(8,128)(2,1)S(1)} %get-tuple-element.28.table_ref, bf16[8,8,128,128]{3,2,1,0:T(8,128)(2,1)S(1)} %copy-done, bf16[1024,512]{1,0:T(8,128)(2,1)S(1)} %copy-done.2, ...), custom_call_target="tpu_custom_call" | custom-call | flops 1610612736 | bytes 5242880 | tf_op jit(solution)/shard_map/pallas_call | solution.py:532
  40.1 1.8 %collective-permute-start.24 = (bf16[64,512]{1,0:T(8,128)(2,1)S(1)}, bf16[64,512]{1,0:T(8,128)(2,1)S(1)}, u32[]{:S(2)}, u32[]{:S(2)}) collective-permute-start(bf16[64,512]{1,0:T(8,128)(2,1)S(1)} %pad_maximum_fusion.7), channel_id=1, source_target_pairs={{0,16},{1,17},{2,18},{3,19},{4,20},{5,21},{6,22},{7,23},{8,24},{9,... | collective-permute-start | bytes 196616 | tf_op jit(solution)/shard_map/ppermute | solution.py:70
  42.1 1.5 %collective-permute-start.9 = (bf16[128,512]{1,0:T(8,128)(2,1)S(1)}, bf16[128,512]{1,0:T(8,128)(2,1)S(1)}, u32[]{:S(2)}, u32[]{:S(2)}) collective-permute-start(bf16[128,512]{1,0:T(8,128)(2,1)S(1)} %get-tuple-element.41), channel_id=1, source_target_pairs={{0,4},{1,9},{2,6},{3,11},{4,0},{5,13},{6,2},{7,15},{8,12},{9,1},{1... | collective-permute-start | bytes 393224 | tf_op jit(solution)/shard_map/ppermute | solution.py:70
  44.2 1.4 %collective-permute-start.11 = (bf16[128,512]{1,0:T(8,128)(2,1)S(1)}, bf16[128,512]{1,0:T(8,128)(2,1)S(1)}, u32[]{:S(2)}, u32[]{:S(2)}) collective-permute-start(bf16[128,512]{1,0:T(8,128)(2,1)S(1)} %get-tuple-element.43), channel_id=1, source_target_pairs={{0,2},{1,17},{2,0},{3,19},{4,6},{5,21},{6,4},{7,23},{8,10},{9,25},... | collective-permute-start | bytes 393224 | tf_op jit(solution)/shard_map/ppermute | solution.py:70
  45.6 2.4 %collective-permute-start.25 = (bf16[64,512]{1,0:T(8,128)(2,1)S(1)}, bf16[64,512]{1,0:T(8,128)(2,1)S(1)}, u32[]{:S(2)}, u32[]{:S(2)}) collective-permute-start(bf16[64,512]{1,0:T(8,128)(2,1)S(1)} %pad_maximum_fusion.8), channel_id=1, source_target_pairs={{0,24},{1,25},{2,26},{3,27},{4,28},{5,29},{6,30},{7,31},{8,16},{9,... | collective-permute-start | bytes 196616 | tf_op jit(solution)/shard_map/ppermute | solution.py:70
  48.0 1.6 %collective-permute-done.13 = bf16[128,512]{1,0:T(8,128)(2,1)S(1)} collective-permute-done((bf16[128,512]{1,0:T(8,128)(2,1)S(1)}, bf16[128,512]{1,0:T(8,128)(2,1)S(1)}, u32[]{:S(2)}, u32[]{:S(2)}) %collective-permute-start.13) | collective-permute-done | bytes 131104 | tf_op jit(solution)/shard_map/ppermute | solution.py:70
  50.7 2.1 %collective-permute-start.16 = (bf16[32,512]{1,0:T(8,128)(2,1)S(1)}, bf16[32,512]{1,0:T(8,128)(2,1)S(1)}, u32[]{:S(2)}, u32[]{:S(2)}) collective-permute-start(bf16[32,512]{1,0:T(8,128)(2,1)S(1)} %get-tuple-element.52), channel_id=1, source_target_pairs={{0,24},{1,7},{2,26},{3,5},{4,28},{5,3},{6,30},{7,1},{8,16},{9,15},... | collective-permute-start | bytes 98312 | tf_op jit(solution)/shard_map/ppermute | solution.py:70
  53.0 2.2 %collective-permute-start.14 = (bf16[32,512]{1,0:T(8,128)(2,1)S(1)}, bf16[32,512]{1,0:T(8,128)(2,1)S(1)}, u32[]{:S(2)}, u32[]{:S(2)}) collective-permute-start(bf16[32,512]{1,0:T(8,128)(2,1)S(1)} %get-tuple-element.54), channel_id=1, source_target_pairs={{0,8},{1,5},{2,10},{3,7},{4,12},{5,1},{6,14},{7,3},{8,0},{9,13},{1... | collective-permute-start | bytes 98312 | tf_op jit(solution)/shard_map/ppermute | solution.py:70
  55.2 1.3 %collective-permute-done.16.refs_3_ = bf16[32,512]{1,0:T(8,128)(2,1)S(1)} collective-permute-done((bf16[32,512]{1,0:T(8,128)(2,1)S(1)}, bf16[32,512]{1,0:T(8,128)(2,1)S(1)}, u32[]{:S(2)}, u32[]{:S(2)}) %collective-permute-start.16) | collective-permute-done | bytes 32800 | tf_op jit(solution)/shard_map/ppermute | solution.py:70
  56.5 1.2 %collective-permute-done.15.refs_2_ = bf16[32,512]{1,0:T(8,128)(2,1)S(1)} collective-permute-done((bf16[32,512]{1,0:T(8,128)(2,1)S(1)}, bf16[32,512]{1,0:T(8,128)(2,1)S(1)}, u32[]{:S(2)}, u32[]{:S(2)}) %collective-permute-start.15) | collective-permute-done | bytes 32800 | tf_op jit(solution)/shard_map/ppermute | solution.py:70
  57.8 1.9 %collective-permute-start.19 = (bf16[32,512]{1,0:T(8,128)(2,1)S(1)}, bf16[32,512]{1,0:T(8,128)(2,1)S(1)}, u32[]{:S(2)}, u32[]{:S(2)}) collective-permute-start(bf16[32,512]{1,0:T(8,128)(2,1)S(1)} %shard_map.144), channel_id=1, source_target_pairs={{0,24},{1,7},{2,26},{3,5},{4,28},{5,3},{6,30},{7,1},{8,16},{9,15},... | collective-permute-start | bytes 98312 | tf_op jit(solution)/shard_map/ppermute | solution.py:70
  60.7 1.5 %collective-permute-start.17 = (bf16[32,512]{1,0:T(8,128)(2,1)S(1)}, bf16[32,512]{1,0:T(8,128)(2,1)S(1)}, u32[]{:S(2)}, u32[]{:S(2)}) collective-permute-start(bf16[32,512]{1,0:T(8,128)(2,1)S(1)} %shard_map.144), channel_id=1, source_target_pairs={{0,8},{1,5},{2,10},{3,7},{4,12},{5,1},{6,14},{7,3},{8,0},{9,13},{1... | collective-permute-start | bytes 98312 | tf_op jit(solution)/shard_map/ppermute | solution.py:70
  62.2 1.3 %collective-permute-done.19 = bf16[32,512]{1,0:T(8,128)(2,1)S(1)} collective-permute-done((bf16[32,512]{1,0:T(8,128)(2,1)S(1)}, bf16[32,512]{1,0:T(8,128)(2,1)S(1)}, u32[]{:S(2)}, u32[]{:S(2)}) %collective-permute-start.19) | collective-permute-done | bytes 32800 | tf_op jit(solution)/shard_map/ppermute | solution.py:70
  63.6 1.3 %collective-permute-done.18 = bf16[32,512]{1,0:T(8,128)(2,1)S(1)} collective-permute-done((bf16[32,512]{1,0:T(8,128)(2,1)S(1)}, bf16[32,512]{1,0:T(8,128)(2,1)S(1)}, u32[]{:S(2)}, u32[]{:S(2)}) %collective-permute-start.18) | collective-permute-done | bytes 32800 | tf_op jit(solution)/shard_map/ppermute | solution.py:70
  64.8 2.0 %collective-permute-start.22 = (bf16[128,512]{1,0:T(8,128)(2,1)S(1)}, bf16[128,512]{1,0:T(8,128)(2,1)S(1)}, u32[]{:S(2)}, u32[]{:S(2)}) collective-permute-start(bf16[128,512]{1,0:T(8,128)(2,1)S(1)} %pad_maximum_fusion.1), channel_id=1, source_target_pairs={{0,6},{1,25},{2,4},{3,27},{4,2},{5,29},{6,0},{7,31},{8,14},{9,17},... | collective-permute-start | bytes 393224 | tf_op jit(solution)/shard_map/ppermute | solution.py:70
  68.4 4.0 %collective-permute-done.20 = bf16[128,512]{1,0:T(8,128)(2,1)S(1)} collective-permute-done((bf16[128,512]{1,0:T(8,128)(2,1)S(1)}, bf16[128,512]{1,0:T(8,128)(2,1)S(1)}, u32[]{:S(2)}, u32[]{:S(2)}) %collective-permute-start.20) | collective-permute-done | bytes 131104 | tf_op jit(solution)/shard_map/ppermute | solution.py:70
  73.0 1.7 %collective-permute-start.26 = (bf16[128,512]{1,0:T(8,128)(2,1)S(1)}, bf16[128,512]{1,0:T(8,128)(2,1)S(1)}, u32[]{:S(2)}, u32[]{:S(2)}) collective-permute-start(bf16[128,512]{1,0:T(8,128)(2,1)S(1)} %pad_maximum_fusion.2), channel_id=1, source_target_pairs={{0,4},{1,5},{2,6},{3,7},{4,0},{5,1},{6,2},{7,3},{8,12},{9,13},{10,... | collective-permute-start | bytes 393224 | tf_op jit(solution)/shard_map/ppermute | solution.py:70
  74.7 1.7 %shard_map.143 = bf16[1024,512]{1,0:T(8,128)(2,1)} custom-call(bf16[1024,512]{1,0:T(8,128)(2,1)S(1)} %get-tuple-element.30.p_ref, bf16[512,512]{1,0:T(8,128)(2,1)S(1)} %constant_dynamic-update-slice_fusion.13.lo_ref, bf16[512,512]{1,0:T(8,128)(2,1)S(1)} %collective-permute-done.6.hi_ref), custom_call_target="tpu_custom_call" | custom-call | flops 536870912 | bytes 2097152 | tf_op jit(solution)/shard_map/pallas_call | solution.py:542
  76.5 2.1 %collective-permute-done.26 = bf16[128,512]{1,0:T(8,128)(2,1)S(1)} collective-permute-done((bf16[128,512]{1,0:T(8,128)(2,1)S(1)}, bf16[128,512]{1,0:T(8,128)(2,1)S(1)}, u32[]{:S(2)}, u32[]{:S(2)}) %collective-permute-start.26) | collective-permute-done | bytes 131104 | tf_op jit(solution)/shard_map/ppermute | solution.py:70
  79.3 1.3 %shard_map.145 = (bf16[2,512,512]{2,1,0:T(8,128)(2,1)}, bf16[128,512]{1,0:T(8,128)(2,1)}, bf16[128,512]{1,0:T(8,128)(2,1)}) custom-call(bf16[512,512]{1,0:T(8,128)(2,1)S(1)} %constant_dynamic-update-slice_fusion.19.part_ref, bf16[256,512]{1,0:T(8,128)(2,1)S(1)} %constant_dynamic-update-slice_fusion.26.fresh_ref), custom_call_target="tpu_custom_call" | custom-call | bytes 1048576 | tf_op jit(solution)/shard_map/pallas_call | solution.py:569
  (91 shorter events, 9.7 us)
Async XLA Ops:
  0.6 23.6 %copy-start.9 = (s32[8,8]{1,0:T(8,128)S(1)}, s32[8,8]{1,0:T(8,128)}, u32[]{:S(2)}) copy-start(s32[8,8]{1,0:T(8,128)} %src_ref.5) | copy-start | bytes 772
  2.4 25.4 %copy-start = (bf16[8,8,128,128]{3,2,1,0:T(8,128)(2,1)S(1)}, bf16[8,8,128,128]{3,2,1,0:T(8,128)(2,1)}, u32[]{:S(2)}) copy-start(bf16[8,8,128,128]{3,2,1,0:T(8,128)(2,1)} %tile_ref.3) | copy-start | bytes 6291460
  2.4 25.4 %copy-start.1 = (bf16[1024,512]{1,0:T(8,128)(2,1)S(1)}, bf16[1024,512]{1,0:T(8,128)(2,1)}, u32[]{:S(2)}) copy-start(bf16[1024,512]{1,0:T(8,128)(2,1)} %feat_ref.1) | copy-start | bytes 3145732
  2.5 10.8 %collective-permute-start.2 = (bf16[64,512]{1,0:T(8,128)(2,1)S(1)}, bf16[64,512]{1,0:T(8,128)(2,1)S(1)}, u32[]{:S(2)}, u32[]{:S(2)}) collective-permute-start(bf16[64,512]{1,0:T(8,128)(2,1)S(1)} %get-tuple-element.87), channel_id=1, source_target_pairs={{0,24},{1,25},{2,26},{3,27},{4,28},{5,29},{6,30},{7,31},{8,16},{9,... | collective-permute-start | bytes 196616 | tf_op jit(solution)/shard_map/ppermute | solution.py:70
  7.6 5.6 %collective-permute-start.1 = (bf16[64,512]{1,0:T(8,128)(2,1)S(1)}, bf16[64,512]{1,0:T(8,128)(2,1)S(1)}, u32[]{:S(2)}, u32[]{:S(2)}) collective-permute-start(bf16[64,512]{1,0:T(8,128)(2,1)S(1)} %get-tuple-element.88), channel_id=1, source_target_pairs={{0,16},{1,17},{2,18},{3,19},{4,20},{5,21},{6,22},{7,23},{8,24},{9,... | collective-permute-start | bytes 196616 | tf_op jit(solution)/shard_map/ppermute | solution.py:70
  7.6 4.3 %collective-permute-start = (bf16[64,512]{1,0:T(8,128)(2,1)S(1)}, bf16[64,512]{1,0:T(8,128)(2,1)S(1)}, u32[]{:S(2)}, u32[]{:S(2)}) collective-permute-start(bf16[64,512]{1,0:T(8,128)(2,1)S(1)} %get-tuple-element.89), channel_id=1, source_target_pairs={{0,8},{1,9},{2,10},{3,11},{4,12},{5,13},{6,14},{7,15},{8,0},{9,1},... | collective-permute-start | bytes 196616 | tf_op jit(solution)/shard_map/ppermute | solution.py:70
  13.3 7.8 %collective-permute-start.3 = (bf16[192,512]{1,0:T(8,128)(2,1)S(1)}, bf16[192,512]{1,0:T(8,128)(2,1)S(1)}, u32[]{:S(2)}, u32[]{:S(2)}) collective-permute-start(bf16[192,512]{1,0:T(8,128)(2,1)S(1)} %get-tuple-element.79), channel_id=1, source_target_pairs={{0,4},{1,5},{2,6},{3,7},{4,0},{5,1},{6,2},{7,3},{8,12},{9,13},{10,... | collective-permute-start | bytes 589832 | tf_op jit(solution)/shard_map/ppermute | solution.py:70
  14.9 9.2 %collective-permute-start.5 = (bf16[128,512]{1,0:T(8,128)(2,1)S(1)}, bf16[128,512]{1,0:T(8,128)(2,1)S(1)}, u32[]{:S(2)}, u32[]{:S(2)}) collective-permute-start(bf16[128,512]{1,0:T(8,128)(2,1)S(1)} %pad_maximum_fusion), channel_id=1, source_target_pairs={{0,6},{1,7},{2,4},{3,5},{4,2},{5,3},{6,0},{7,1},{8,14},{9,15},{10,... | collective-permute-start | bytes 393224 | tf_op jit(solution)/shard_map/ppermute | solution.py:70
  16.4 7.6 %collective-permute-start.4 = (bf16[128,512]{1,0:T(8,128)(2,1)S(1)}, bf16[128,512]{1,0:T(8,128)(2,1)S(1)}, u32[]{:S(2)}, u32[]{:S(2)}) collective-permute-start(bf16[128,512]{1,0:T(8,128)(2,1)S(1)} %pad_maximum_fusion), channel_id=1, source_target_pairs={{0,2},{1,3},{2,0},{3,1},{4,6},{5,7},{6,4},{7,5},{8,10},{9,11},{10,... | collective-permute-start | bytes 393224 | tf_op jit(solution)/shard_map/ppermute | solution.py:70
  24.1 5.9 %collective-permute-start.6 = (bf16[512,512]{1,0:T(8,128)(2,1)S(1)}, bf16[512,512]{1,0:T(8,128)(2,1)S(1)}, u32[]{:S(2)}, u32[]{:S(2)}) collective-permute-start(bf16[512,512]{1,0:T(8,128)(2,1)S(1)} %constant_dynamic-update-slice_fusion.13.lo_ref), channel_id=1, source_target_pairs={{0,1},{1,0},{2,3},{3,2},{4,5},{5,4},{6,7},{7,6},{8,9},{9,8},{10,11... | collective-permute-start | bytes 1572872 | tf_op jit(solution)/shard_map/ppermute | solution.py:70
  36.2 8.0 %collective-permute-start.23 = (bf16[64,512]{1,0:T(8,128)(2,1)S(1)}, bf16[64,512]{1,0:T(8,128)(2,1)S(1)}, u32[]{:S(2)}, u32[]{:S(2)}) collective-permute-start(bf16[64,512]{1,0:T(8,128)(2,1)S(1)} %pad_maximum_fusion.6), channel_id=1, source_target_pairs={{0,8},{1,9},{2,10},{3,11},{4,12},{5,13},{6,14},{7,15},{8,0},{9,1},... | collective-permute-start | bytes 196616 | tf_op jit(solution)/shard_map/ppermute | solution.py:70
  39.0 18.7 %copy-start.3 = (f32[2,16,512]{2,1,0:T(8,128)S(1)}, f32[2,16,512]{2,1,0:T(8,128)}, u32[]{:S(2)}) copy-start(f32[2,16,512]{2,1,0:T(8,128)} %refs_4_.3) | copy-start | bytes 196612
  39.0 2.8 %collective-permute-start.12 = (bf16[128,512]{1,0:T(8,128)(2,1)S(1)}, bf16[128,512]{1,0:T(8,128)(2,1)S(1)}, u32[]{:S(2)}, u32[]{:S(2)}) collective-permute-start(bf16[128,512]{1,0:T(8,128)(2,1)S(1)} %get-tuple-element.38), channel_id=1, source_target_pairs={{0,1},{1,0},{2,3},{3,2},{4,5},{5,4},{6,7},{7,6},{8,9},{9,8},{10,11... | collective-permute-start | bytes 393224 | tf_op jit(solution)/shard_map/ppermute | solution.py:70
  39.6 2.4 %collective-permute-start.10 = (bf16[128,512]{1,0:T(8,128)(2,1)S(1)}, bf16[128,512]{1,0:T(8,128)(2,1)S(1)}, u32[]{:S(2)}, u32[]{:S(2)}) collective-permute-start(bf16[128,512]{1,0:T(8,128)(2,1)S(1)} %get-tuple-element.39), channel_id=1, source_target_pairs={{0,1},{1,0},{2,3},{3,2},{4,5},{5,4},{6,7},{7,6},{8,9},{9,8},{10,11... | collective-permute-start | bytes 393224 | tf_op jit(solution)/shard_map/ppermute | solution.py:70
  39.6 2.3 %collective-permute-start.8 = (bf16[128,512]{1,0:T(8,128)(2,1)S(1)}, bf16[128,512]{1,0:T(8,128)(2,1)S(1)}, u32[]{:S(2)}, u32[]{:S(2)}) collective-permute-start(bf16[128,512]{1,0:T(8,128)(2,1)S(1)} %get-tuple-element.40), channel_id=1, source_target_pairs={{0,1},{1,0},{2,3},{3,2},{4,5},{5,4},{6,7},{7,6},{8,9},{9,8},{10,11... | collective-permute-start | bytes 393224 | tf_op jit(solution)/shard_map/ppermute | solution.py:70
  40.1 15.1 %collective-permute-start.24 = (bf16[64,512]{1,0:T(8,128)(2,1)S(1)}, bf16[64,512]{1,0:T(8,128)(2,1)S(1)}, u32[]{:S(2)}, u32[]{:S(2)}) collective-permute-start(bf16[64,512]{1,0:T(8,128)(2,1)S(1)} %pad_maximum_fusion.7), channel_id=1, source_target_pairs={{0,16},{1,17},{2,18},{3,19},{4,20},{5,21},{6,22},{7,23},{8,24},{9,... | collective-permute-start | bytes 196616 | tf_op jit(solution)/shard_map/ppermute | solution.py:70
  41.9 3.8 %collective-permute-start.7 = (bf16[128,512]{1,0:T(8,128)(2,1)S(1)}, bf16[128,512]{1,0:T(8,128)(2,1)S(1)}, u32[]{:S(2)}, u32[]{:S(2)}) collective-permute-start(bf16[128,512]{1,0:T(8,128)(2,1)S(1)} %get-tuple-element.37), channel_id=1, source_target_pairs={{0,1},{1,0},{2,3},{3,2},{4,5},{5,4},{6,7},{7,6},{8,9},{9,8},{10,11... | collective-permute-start | bytes 393224 | tf_op jit(solution)/shard_map/ppermute | solution.py:70
  42.1 6.0 %collective-permute-start.9 = (bf16[128,512]{1,0:T(8,128)(2,1)S(1)}, bf16[128,512]{1,0:T(8,128)(2,1)S(1)}, u32[]{:S(2)}, u32[]{:S(2)}) collective-permute-start(bf16[128,512]{1,0:T(8,128)(2,1)S(1)} %get-tuple-element.41), channel_id=1, source_target_pairs={{0,4},{1,9},{2,6},{3,11},{4,0},{5,13},{6,2},{7,15},{8,12},{9,1},{1... | collective-permute-start | bytes 393224 | tf_op jit(solution)/shard_map/ppermute | solution.py:70
  43.6 6.0 %collective-permute-start.13 = (bf16[128,512]{1,0:T(8,128)(2,1)S(1)}, bf16[128,512]{1,0:T(8,128)(2,1)S(1)}, u32[]{:S(2)}, u32[]{:S(2)}) collective-permute-start(bf16[128,512]{1,0:T(8,128)(2,1)S(1)} %get-tuple-element.42), channel_id=1, source_target_pairs={{0,6},{1,25},{2,4},{3,27},{4,2},{5,29},{6,0},{7,31},{8,14},{9,17},... | collective-permute-start | bytes 393224 | tf_op jit(solution)/shard_map/ppermute | solution.py:70
  44.2 6.4 %collective-permute-start.11 = (bf16[128,512]{1,0:T(8,128)(2,1)S(1)}, bf16[128,512]{1,0:T(8,128)(2,1)S(1)}, u32[]{:S(2)}, u32[]{:S(2)}) collective-permute-start(bf16[128,512]{1,0:T(8,128)(2,1)S(1)} %get-tuple-element.43), channel_id=1, source_target_pairs={{0,2},{1,17},{2,0},{3,19},{4,6},{5,21},{6,4},{7,23},{8,10},{9,25},... | collective-permute-start | bytes 393224 | tf_op jit(solution)/shard_map/ppermute | solution.py:70
  45.6 27.3 %collective-permute-start.25 = (bf16[64,512]{1,0:T(8,128)(2,1)S(1)}, bf16[64,512]{1,0:T(8,128)(2,1)S(1)}, u32[]{:S(2)}, u32[]{:S(2)}) collective-permute-start(bf16[64,512]{1,0:T(8,128)(2,1)S(1)} %pad_maximum_fusion.8), channel_id=1, source_target_pairs={{0,24},{1,25},{2,26},{3,27},{4,28},{5,29},{6,30},{7,31},{8,16},{9,... | collective-permute-start | bytes 196616 | tf_op jit(solution)/shard_map/ppermute | solution.py:70
  50.7 5.8 %collective-permute-start.16 = (bf16[32,512]{1,0:T(8,128)(2,1)S(1)}, bf16[32,512]{1,0:T(8,128)(2,1)S(1)}, u32[]{:S(2)}, u32[]{:S(2)}) collective-permute-start(bf16[32,512]{1,0:T(8,128)(2,1)S(1)} %get-tuple-element.52), channel_id=1, source_target_pairs={{0,24},{1,7},{2,26},{3,5},{4,28},{5,3},{6,30},{7,1},{8,16},{9,15},... | collective-permute-start | bytes 98312 | tf_op jit(solution)/shard_map/ppermute | solution.py:70
  52.9 4.8 %collective-permute-start.15 = (bf16[32,512]{1,0:T(8,128)(2,1)S(1)}, bf16[32,512]{1,0:T(8,128)(2,1)S(1)}, u32[]{:S(2)}, u32[]{:S(2)}) collective-permute-start(bf16[32,512]{1,0:T(8,128)(2,1)S(1)} %get-tuple-element.53), channel_id=1, source_target_pairs={{0,16},{1,3},{2,18},{3,1},{4,20},{5,7},{6,22},{7,5},{8,24},{9,11},... | collective-permute-start | bytes 98312 | tf_op jit(solution)/shard_map/ppermute | solution.py:70
  53.0 4.7 %collective-permute-start.14 = (bf16[32,512]{1,0:T(8,128)(2,1)S(1)}, bf16[32,512]{1,0:T(8,128)(2,1)S(1)}, u32[]{:S(2)}, u32[]{:S(2)}) collective-permute-start(bf16[32,512]{1,0:T(8,128)(2,1)S(1)} %get-tuple-element.54), channel_id=1, source_target_pairs={{0,8},{1,5},{2,10},{3,7},{4,12},{5,1},{6,14},{7,3},{8,0},{9,13},{1... | collective-permute-start | bytes 98312 | tf_op jit(solution)/shard_map/ppermute | solution.py:70
  57.8 5.8 %collective-permute-start.19 = (bf16[32,512]{1,0:T(8,128)(2,1)S(1)}, bf16[32,512]{1,0:T(8,128)(2,1)S(1)}, u32[]{:S(2)}, u32[]{:S(2)}) collective-permute-start(bf16[32,512]{1,0:T(8,128)(2,1)S(1)} %shard_map.144), channel_id=1, source_target_pairs={{0,24},{1,7},{2,26},{3,5},{4,28},{5,3},{6,30},{7,1},{8,16},{9,15},... | collective-permute-start | bytes 98312 | tf_op jit(solution)/shard_map/ppermute | solution.py:70
  59.7 5.2 %collective-permute-start.18 = (bf16[32,512]{1,0:T(8,128)(2,1)S(1)}, bf16[32,512]{1,0:T(8,128)(2,1)S(1)}, u32[]{:S(2)}, u32[]{:S(2)}) collective-permute-start(bf16[32,512]{1,0:T(8,128)(2,1)S(1)} %shard_map.144), channel_id=1, source_target_pairs={{0,16},{1,3},{2,18},{3,1},{4,20},{5,7},{6,22},{7,5},{8,24},{9,11},... | collective-permute-start | bytes 98312 | tf_op jit(solution)/shard_map/ppermute | solution.py:70
  60.7 4.1 %collective-permute-start.17 = (bf16[32,512]{1,0:T(8,128)(2,1)S(1)}, bf16[32,512]{1,0:T(8,128)(2,1)S(1)}, u32[]{:S(2)}, u32[]{:S(2)}) collective-permute-start(bf16[32,512]{1,0:T(8,128)(2,1)S(1)} %shard_map.144), channel_id=1, source_target_pairs={{0,8},{1,5},{2,10},{3,7},{4,12},{5,1},{6,14},{7,3},{8,0},{9,13},{1... | collective-permute-start | bytes 98312 | tf_op jit(solution)/shard_map/ppermute | solution.py:70
  64.8 7.6 %collective-permute-start.22 = (bf16[128,512]{1,0:T(8,128)(2,1)S(1)}, bf16[128,512]{1,0:T(8,128)(2,1)S(1)}, u32[]{:S(2)}, u32[]{:S(2)}) collective-permute-start(bf16[128,512]{1,0:T(8,128)(2,1)S(1)} %pad_maximum_fusion.1), channel_id=1, source_target_pairs={{0,6},{1,25},{2,4},{3,27},{4,2},{5,29},{6,0},{7,31},{8,14},{9,17},... | collective-permute-start | bytes 393224 | tf_op jit(solution)/shard_map/ppermute | solution.py:70
  66.9 5.6 %collective-permute-start.21 = (bf16[128,512]{1,0:T(8,128)(2,1)S(1)}, bf16[128,512]{1,0:T(8,128)(2,1)S(1)}, u32[]{:S(2)}, u32[]{:S(2)}) collective-permute-start(bf16[128,512]{1,0:T(8,128)(2,1)S(1)} %pad_maximum_fusion.1), channel_id=1, source_target_pairs={{0,2},{1,17},{2,0},{3,19},{4,6},{5,21},{6,4},{7,23},{8,10},{9,25},... | collective-permute-start | bytes 393224 | tf_op jit(solution)/shard_map/ppermute | solution.py:70
  67.4 5.0 %collective-permute-start.20 = (bf16[128,512]{1,0:T(8,128)(2,1)S(1)}, bf16[128,512]{1,0:T(8,128)(2,1)S(1)}, u32[]{:S(2)}, u32[]{:S(2)}) collective-permute-start(bf16[128,512]{1,0:T(8,128)(2,1)S(1)} %pad_maximum_fusion.1), channel_id=1, source_target_pairs={{0,4},{1,9},{2,6},{3,11},{4,0},{5,13},{6,2},{7,15},{8,12},{9,1},{1... | collective-permute-start | bytes 393224 | tf_op jit(solution)/shard_map/ppermute | solution.py:70
  72.5 8.1 %collective-permute-start.27 = (bf16[512,512]{1,0:T(8,128)(2,1)S(1)}, bf16[512,512]{1,0:T(8,128)(2,1)S(1)}, u32[]{:S(2)}, u32[]{:S(2)}) collective-permute-start(bf16[512,512]{1,0:T(8,128)(2,1)S(1)} %constant_dynamic-update-slice_fusion.19.part_ref), channel_id=1, source_target_pairs={{0,1},{1,0},{2,3},{3,2},{4,5},{5,4},{6,7},{7,6},{8,9},{9,8},{10,11... | collective-permute-start | bytes 1572872 | tf_op jit(solution)/shard_map/ppermute | solution.py:70
  73.0 5.6 %collective-permute-start.26 = (bf16[128,512]{1,0:T(8,128)(2,1)S(1)}, bf16[128,512]{1,0:T(8,128)(2,1)S(1)}, u32[]{:S(2)}, u32[]{:S(2)}) collective-permute-start(bf16[128,512]{1,0:T(8,128)(2,1)S(1)} %pad_maximum_fusion.2), channel_id=1, source_target_pairs={{0,4},{1,5},{2,6},{3,7},{4,0},{5,1},{6,2},{7,3},{8,12},{9,13},{10,... | collective-permute-start | bytes 393224 | tf_op jit(solution)/shard_map/ppermute | solution.py:70
  (6 other events, 47.6 us)
